TPU v7x, 256 devices: a whole 4x4x8 slice. The times are simulated.
256 devices in a mesh: seq: 128 (over x, y, z), head: 2 (over core).
Axes of the slice: x: 4, y: 4, z: 8, core: 2. Of those that a mesh axis runs over, the one named last changes fastest.
Arguments:
- tiles: bfloat16 [16384, 768], P('seq', 'head'), may hold values from -6 to 6
- ln_gain: float32 [768], replicated, may hold values from 0.25 to 1.75
- w_qkv: bfloat16 [768, 3, 768], P(None, None, 'head'), as said below
- w_out: bfloat16 [768, 768], P('head'), may hold values from -0.21875 to 0.21875
- tile_source: int32 [16384], P('seq'), may hold values from 0 to 16383, as said below
- tissue_count: int32 [128], P('seq'), may hold values from 64 to 128
Outputs:
- encoded: bfloat16 [16384, 768], P('seq', 'head')
Inputs may be any that keep to these rules, and one draw needn't show every extreme that they name: `tile_source`: A permutation of the 16384 rows; exactly one tile goes to Hilbert block d from each encoder block s, namely row s * 128 + d; within block d these 128 tiles come in any order. `w_qkv`: projection weights; the query third may be larger than the key and value thirds.
All inputs are finite; a program needn't handle non-finite values.
Results may differ from a plain program's by a relative error of at most 0.0095.
The roundings to bfloat16 on the way count: a program that leaves them out, or rounds other values in their place, can miss the bound.
Values may be sent and summed in bfloat16 or wider, within the bound.
A program may use at most 64 MiB of HBM per device.

v0:
```python
import jax
import jax.numpy as jnp
from jax import lax
from jax.sharding import PartitionSpec as P

D = 768
HEAD_DIM = 64
SPAN_SHORT = 4
MIDDLE_SPAN = 16
MIDDLE_DILATION = 4
WHOLE_DILATION = 16


masked_score = -1e30


def shortened(value):

    def short(part):
        return part.astype(jnp.bfloat16) if part.dtype == jnp.float32 else part

    return jax.tree.map(short, value)


def swapped(value, axis, apart):
    return lax.ppermute(value, axis, [(i, i ^ 1 << apart) for i in range(lax.axis_size(axis))])


def absorb(softmax_state, queries, key_matrix, value_matrix, key_live):
    running_max, running_sum, weighted = softmax_state
    scores = jnp.einsum(
        "qhd,khd->hqk", queries, key_matrix, preferred_element_type=jnp.float32
    ) * queries.shape[-1] ** (-0.5)
    scores = jnp.where(key_live.T[:, None, :] > 0.5, scores, masked_score)
    new_max = jnp.maximum(running_max, jnp.max(scores, axis=-1))
    rescale = jnp.exp(running_max - new_max)
    probability = jnp.exp(scores - new_max[..., None])
    running_sum = running_sum * rescale + jnp.sum(probability, axis=-1)
    mixed = jnp.einsum(
        "hqk,khd->qhd",
        probability.astype(jnp.bfloat16),
        value_matrix,
        preferred_element_type=jnp.float32,
    )
    weighted = weighted * rescale.T[:, :, None] + mixed
    return (new_max, running_sum, weighted)


def select_rows(key_matrix, value_matrix, row_active_mask, stride, offsets):
    kept_rows = key_matrix.shape[0] // stride
    heads_local = key_matrix.shape[1]
    selector = jnp.broadcast_to(
        offsets[None, None, :, None], (kept_rows, 1, heads_local, key_matrix.shape[2])
    )
    picked_keys = jnp.take_along_axis(
        key_matrix.reshape(kept_rows, stride, heads_local, key_matrix.shape[2]), selector, axis=1
    )[:, 0]
    picked_values = jnp.take_along_axis(
        value_matrix.reshape(kept_rows, stride, heads_local, value_matrix.shape[2]),
        selector,
        axis=1,
    )[:, 0]
    picked_live = row_active_mask.reshape(kept_rows, stride)[:, offsets]
    return (picked_keys, picked_values, picked_live)


def join_parts(local_part, remote_part):
    return tuple(
        (
            jnp.concatenate((mine_rows, their_rows), 0)
            for mine_rows, their_rows in zip(local_part, remote_part)
        )
    )


def absorb_blocks(softmax_state, queries, members, step_rows):
    for offset_row in range(0, members[0].shape[0], step_rows):
        softmax_state = absorb(
            softmax_state,
            queries,
            *[member[offset_row : offset_row + step_rows] for member in members]
        )
    return softmax_state


def shards(tiles, ln_gain, w_qkv, w_out, tile_source, tissue_count):
    tok_rows = tiles.shape[0]
    blocks = lax.axis_size("seq")
    per_peer = tok_rows // blocks
    arrival = tile_source // tok_rows * per_peer + tile_source % per_peer
    whole_rows = lax.all_gather(tiles, "head", axis=1, tiled=True)
    arrived = lax.all_to_all(
        whole_rows.reshape(blocks, per_peer, whole_rows.shape[1]),
        "seq",
        split_axis=0,
        concat_axis=0,
        tiled=True,
    )
    relaid = arrived.reshape(tok_rows, whole_rows.shape[1])[arrival]
    widened = relaid.astype(jnp.float32)
    row_mean = jnp.mean(widened, axis=-1, keepdims=True)
    centered = widened - row_mean
    row_var = jnp.mean(centered * centered, axis=-1, keepdims=True)
    normed = (centered * lax.rsqrt(row_var + 1e-05) * ln_gain).astype(jnp.bfloat16)
    heads_local = w_qkv.shape[2] // HEAD_DIM
    packed = jnp.dot(
        normed, w_qkv.reshape(D, 3 * w_qkv.shape[2]), preferred_element_type=jnp.float32
    ).astype(jnp.bfloat16)
    packed = packed.reshape(tok_rows, 3, heads_local, HEAD_DIM)
    queries, key_matrix, value_matrix = (packed[:, 0], packed[:, 1], packed[:, 2])
    row_active_mask = (jnp.arange(tok_rows, dtype=jnp.int32) < tissue_count[0]).astype(jnp.bfloat16)
    live_all = jnp.broadcast_to(row_active_mask[:, None], (tok_rows, heads_local))
    present_heads = lax.axis_index("head") * heads_local + jnp.arange(heads_local, dtype=jnp.int32)
    softmax_state = (
        jnp.full((heads_local, tok_rows), masked_score, jnp.float32),
        jnp.zeros((heads_local, tok_rows), jnp.float32),
        jnp.zeros((tok_rows, heads_local, HEAD_DIM), jnp.float32),
    )
    gathered = (key_matrix, value_matrix, live_all)
    for level in range(SPAN_SHORT.bit_length() - 1):
        partner = jax.tree.map(
            lambda part, own: part.astype(own.dtype),
            swapped(shortened(gathered), "seq", level),
            gathered,
        )
        gathered = join_parts(gathered, partner)
    softmax_state = absorb(softmax_state, queries, *gathered)
    middle_branch = select_rows(
        key_matrix, value_matrix, row_active_mask, MIDDLE_DILATION, present_heads % MIDDLE_DILATION
    )
    faraway_part = select_rows(
        key_matrix, value_matrix, row_active_mask, WHOLE_DILATION, present_heads % WHOLE_DILATION
    )
    for level in range(MIDDLE_SPAN.bit_length() - 1):
        partner = jax.tree.map(
            lambda part, own: part.astype(own.dtype),
            swapped(shortened(middle_branch), "seq", level),
            middle_branch,
        )
        middle_branch = join_parts(middle_branch, partner)
    softmax_state = absorb(softmax_state, queries, *middle_branch)
    faraway_part = (
        lax.all_gather(faraway_part[0], "seq", axis=0, tiled=True),
        lax.all_gather(faraway_part[1], "seq", axis=0, tiled=True),
        lax.all_gather(faraway_part[2], "seq", axis=0, tiled=True),
    )
    step_rows = min(faraway_part[0].shape[0], middle_branch[0].shape[0])
    softmax_state = absorb_blocks(softmax_state, queries, faraway_part, step_rows)
    running_max, running_sum, weighted = softmax_state
    attended = (
        weighted / running_sum.T[:, :, None] * row_active_mask.astype(jnp.float32)[:, None, None]
    )
    attended = attended.astype(jnp.bfloat16).reshape(tok_rows, heads_local * HEAD_DIM)
    partial_value = jnp.dot(attended, w_out, preferred_element_type=jnp.float32)
    return lax.psum_scatter(
        partial_value.astype(jnp.bfloat16), "head", scatter_dimension=1, tiled=True
    )


def solution(mesh):
    return jax.shard_map(
        shards,
        mesh=mesh,
        in_specs=(
            P("seq", "head"),
            P(),
            P(None, None, "head"),
            P("head", None),
            P("seq"),
            P("seq"),
        ),
        out_specs=P("seq", "head"),
        check_vma=False,
    )
```

profile of v0, /device:TPU:1, one launch (start us, length us, event | category | flops | bytes accessed | tf_op | source)
XLA Modules:
  0.0 1479.4 jit_solution(4829713266391347686)
XLA Ops:
  6.5 5.3 all_gather.12
  11.8 0.5 broadcast.579
  12.4 0.7 reduce
  13.1 0.7 reshape.331
  13.8 13.8 all-to-all-start
  28.3 0.6 gather_fusion.1
  28.9 0.7 collective-permute-start.6
  29.6 0.9 collective-permute-start
  31.2 0.6 gather_fusion.2
  31.7 0.1 copy.105
  31.8 290.8 %all-gather = bf16[1024,6]{1,0:T(8,128)(2,1)S(1)} all-gather(bf16[8,6]{1,0:T(8,128)(2,1)S(1)} %copy.105), channel_id=2, replica_groups=mesh['seq'=128,'head'=2] {'seq'}, dimensions={0}, use_global_device_ids=true | all-gather | bytes 12384 | tf_op jit(solution)/shard_map/all_gather | solution.py:145
  322.6 0.1 copy.125
  322.7 0.1 copy.128
  323.2 2.6 copy.90
  326.0 0.3 collective-permute-done.7
  326.5 2.1 collective-permute-start.1
  328.6 4.2 collective-permute-done.8
  332.9 2.7 collective-permute-done.9
  335.7 0.1 reshape.332
  335.9 0.9 gather_fusion
  336.8 0.1 convert_reduce_fusion
  336.9 0.2 fusion.36
  337.1 0.7 convolution_convert_fusion
  337.9 0.2 copy.91
  338.2 0.2 copy.92
  338.4 130.2 %gather_fusion.3 = bf16[12288]{0:T(1024)(128)(2,1)S(1)} fusion(bf16[32,4,6,64]{3,1,0,2:T(4,128)(2,1)S(1)} %bitcast.224, s32[12288]{0:T(1024)S(1)} %reshape.307), kind=kCustom, calls=%fused_computation.clone | custom fusion | bytes 245760 | tf_op jit(solution)/shard_map/jit(take_along_axis)/gather | solution.py:55
  468.6 0.1 reshape.310
  468.7 0.2 copy.96
  468.9 130.2 %gather_fusion.4 = bf16[12288]{0:T(1024)(128)(2,1)S(1)} fusion(bf16[32,4,6,64]{3,1,0,2:T(4,128)(2,1)S(1)} %bitcast.226, s32[12288]{0:T(1024)S(1)} %reshape.313), kind=kCustom, calls=%fused_computation.2.clone | custom fusion | bytes 245760 | tf_op jit(solution)/shard_map/jit(take_along_axis)/gather | solution.py:58
  599.1 0.1 reshape.316
  599.2 0.7 constant_dynamic-update-slice_fusion.9
  600.0 33.9 %gather_fusion.5 = bf16[3072]{0:T(1024)(128)(2,1)S(1)} fusion(bf16[8,16,6,64]{3,1,0,2:T(8,128)(2,1)S(1)} %bitcast.225, s32[3072]{0:T(1024)S(1)} %reshape.319), kind=kCustom, calls=%fused_computation.1.clone | custom fusion | bytes 61440 | tf_op jit(solution)/shard_map/jit(take_along_axis)/gather | solution.py:55
  633.9 33.9 %gather_fusion.6 = bf16[3072]{0:T(1024)(128)(2,1)S(1)} fusion(bf16[8,16,6,64]{3,1,0,2:T(8,128)(2,1)S(1)} %bitcast.227, s32[3072]{0:T(1024)S(1)} %reshape.319), kind=kCustom, calls=%fused_computation.3.clone | custom fusion | bytes 61440 | tf_op jit(solution)/shard_map/jit(take_along_axis)/gather | solution.py:58
  668.0 292.7 %all-gather.1 = bf16[1024,1,6,64]{3,0,2,1:T(8,128)(2,1)S(1)} all-gather(bf16[8,1,6,64]{3,0,2,1:T(8,128)(2,1)S(1)} %copy.110), channel_id=3, replica_groups=mesh['seq'=128,'head'=2] {'seq'}, dimensions={0}, use_global_device_ids=true | all-gather | bytes 792576 | tf_op jit(solution)/shard_map/all_gather | solution.py:143
  960.7 1.5 collective-permute-start.14
  962.2 291.3 %all-gather.2 = bf16[1024,1,6,64]{3,0,2,1:T(8,128)(2,1)S(1)} all-gather(bf16[8,1,6,64]{3,0,2,1:T(8,128)(2,1)S(1)} %copy.115), channel_id=4, replica_groups=mesh['seq'=128,'head'=2] {'seq'}, dimensions={0}, use_global_device_ids=true | all-gather | bytes 792576 | tf_op jit(solution)/shard_map/all_gather | solution.py:144
  1253.5 0.5 fusion.107
  1254.0 0.5 fusion.106
  1254.5 1.7 collective-permute-start.4
  1256.4 2.4 collective-permute-start.15
  1258.8 6.0 collective-permute-done.11
  1264.9 0.9 collective-permute-done.15
  1265.9 4.5 collective-permute-start.16
  1270.7 2.4 collective-permute-start.5
  1273.1 0.6 collective-permute-done.12
  1273.8 3.3 collective-permute-done.16
  1277.2 0.3 collective-permute-start.17
  1277.6 2.4 collective-permute-done.3
  1280.0 0.5 fusion
  1280.5 0.2 collective-permute-done.13
  1280.8 0.5 fusion.1
  1281.3 0.5 fusion.2
  1281.8 0.6 convolution_bitcast_fusion.2
  1282.4 0.5 fusion.4
  1283.0 0.6 convolution_bitcast_fusion.1
  1283.5 0.5 fusion.8
  1284.1 0.6 collective-permute-done.17
  1284.7 0.7 convolution_bitcast_fusion.3
  1285.4 0.5 fusion.6
  1285.9 0.6 fusion.19
  1286.5 0.3 convolution_convert_fusion.1
  1286.8 0.8 copy.122
  1287.7 183.2 %reduce-scatter.4.cloned.1.call-done = bf16[384,128]{1,0:T(8,128)(2,1)} async-done(((bf16[768,128]{1,0:T(8,128)(2,1)}), bf16[384,128]{1,0:T(8,128)(2,1)}) %reduce-scatter.4.cloned.1.call-update) | async-done | bytes 98320
  1470.9 1.6 copy.123
  (102 shorter events, 2.9 us)
Async XLA Ops:
  6.5 1280.0 %copy-start = (bf16[384,768]{1,0:T(8,128)(2,1)S(1)}, bf16[384,768]{1,0:T(8,128)(2,1)}, u32[]{:S(2)}) copy-start(bf16[384,768]{1,0:T(8,128)(2,1)} %param.13) | copy-start | bytes 1769476
  11.8 18.9 %copy-start.3 = (s32[128]{0:T(128)S(1)}, s32[128]{0:T(128)}, u32[]{:S(2)}) copy-start(s32[128]{0:T(128)} %param.14) | copy-start | bytes 1540
  13.8 321.9 %all-to-all-start = ((bf16[128,2,384]{2,1,0:T(2,128)(2,1)}), bf16[128,2,384]{2,1,0:T(2,128)(2,1)S(1)}, u32[]{:S(2)}, u32[]{:S(2)}) async-start(bf16[128,2,384]{2,1,0:T(2,128)(2,1)} %reshape.331), calls=%async_computation | async-start | bytes 393216 | tf_op jit(solution)/shard_map/all_to_all | solution.py:92
  27.6 1443.3 %reduce-scatter.4.cloned.1.call-start = ((), (), s32[]{:S(2)}) async-start(), calls=%async_computation.2 | async-start | bytes 294912
  28.9 294.0 %collective-permute-start.6 = (bf16[32,6]{0,1:T(8,128)(2,1)S(1)}, bf16[32,6]{0,1:T(8,128)(2,1)S(1)}, u32[]{:S(2)}, u32[]{:S(2)}) collective-permute-start(bf16[32,6]{0,1:T(8,128)(2,1)S(1)} %bitcast.237), channel_id=1, source_target_pairs={{0,2},{2,0},{4,6},{6,4},{8,10},{10,8},{12,14},{14,12},{16,18},{18,... | collective-permute-start | bytes 1160 | tf_op jit(solution)/shard_map/ppermute | solution.py:26
  29.6 296.9 %collective-permute-start = (bf16[128,6]{0,1:T(8,128)(2,1)S(1)}, bf16[128,6]{0,1:T(8,128)(2,1)S(1)}, u32[]{:S(2)}, u32[]{:S(2)}) collective-permute-start(bf16[128,6]{0,1:T(8,128)(2,1)S(1)} %broadcast_in_dim.86), channel_id=1, source_target_pairs={{0,2},{2,0},{4,6},{6,4},{8,10},{10,8},{12,14},{14,12},{16,18},{18,... | collective-permute-start | bytes 4616 | tf_op jit(solution)/shard_map/ppermute | solution.py:26
  323.0 3.4 collective-permute-start.7
  326.4 6.4 collective-permute-start.8
  326.5 6.4 collective-permute-start.1
  332.8 2.8 collective-permute-start.9
  335.7 1.4 copy-start.1
  600.0 656.2 %collective-permute-start.10 = (bf16[32,6,64]{2,0,1:T(8,128)(2,1)S(1)}, bf16[32,6,64]{2,0,1:T(8,128)(2,1)S(1)}, u32[]{:S(2)}, u32[]{:S(2)}) collective-permute-start(bf16[32,6,64]{2,0,1:T(8,128)(2,1)S(1)} %get-tuple-element.27), channel_id=1, source_target_pairs={{0,2},{2,0},{4,6},{6,4},{8,10},{10,8},{12,14},{14,12},{16,18},{18,... | collective-permute-start | bytes 73736 | tf_op jit(solution)/shard_map/ppermute | solution.py:26
  960.7 309.8 %collective-permute-start.2 = (bf16[128,6,64]{0,2,1:T(8,128)(2,1)S(1)}, bf16[128,6,64]{0,2,1:T(8,128)(2,1)S(1)}, u32[]{:S(2)}, u32[]{:S(2)}) collective-permute-start(bf16[128,6,64]{0,2,1:T(8,128)(2,1)S(1)} %get-tuple-element.18), channel_id=1, source_target_pairs={{0,2},{2,0},{4,6},{6,4},{8,10},{10,8},{12,14},{14,12},{16,18},{18,... | collective-permute-start | bytes 294920 | tf_op jit(solution)/shard_map/ppermute | solution.py:26
  960.7 295.6 %collective-permute-start.14 = (bf16[32,6,64]{2,0,1:T(8,128)(2,1)S(1)}, bf16[32,6,64]{2,0,1:T(8,128)(2,1)S(1)}, u32[]{:S(2)}, u32[]{:S(2)}) collective-permute-start(bf16[32,6,64]{2,0,1:T(8,128)(2,1)S(1)} %get-tuple-element.11), channel_id=1, source_target_pairs={{0,2},{2,0},{4,6},{6,4},{8,10},{10,8},{12,14},{14,12},{16,18},{18,... | collective-permute-start | bytes 73736 | tf_op jit(solution)/shard_map/ppermute | solution.py:26
  1254.0 4.8 copy-start.2
  1254.5 16.1 %collective-permute-start.4 = (bf16[128,6,64]{0,2,1:T(8,128)(2,1)S(1)}, bf16[128,6,64]{0,2,1:T(8,128)(2,1)S(1)}, u32[]{:S(2)}, u32[]{:S(2)}) collective-permute-start(bf16[128,6,64]{0,2,1:T(8,128)(2,1)S(1)} %get-tuple-element.17), channel_id=1, source_target_pairs={{0,2},{2,0},{4,6},{6,4},{8,10},{10,8},{12,14},{14,12},{16,18},{18,... | collective-permute-start | bytes 294920 | tf_op jit(solution)/shard_map/ppermute | solution.py:26
  1256.2 8.6 collective-permute-start.11
  1256.4 9.5 collective-permute-start.15
  1264.8 8.8 collective-permute-start.12
  1265.9 11.2 collective-permute-start.16
  1270.5 9.5 collective-permute-start.3
  1270.7 15.3 %collective-permute-start.5 = (bf16[256,6,64]{0,2,1:T(8,128)(2,1)S(1)}, bf16[256,6,64]{0,2,1:T(8,128)(2,1)S(1)}, u32[]{:S(2)}, u32[]{:S(2)}) collective-permute-start(bf16[256,6,64]{0,2,1:T(8,128)(2,1)S(1)} %pad_maximum_fusion.3), channel_id=1, source_target_pairs={{0,4},{2,6},{4,0},{6,2},{8,12},{10,14},{12,8},{14,10},{16,20},{18,... | collective-permute-start | bytes 589832 | tf_op jit(solution)/shard_map/ppermute | solution.py:26
  1273.7 7.0 collective-permute-start.13
  1277.2 7.5 collective-permute-start.17
Sparse Core Ops, SparseCore 0:
  1287.8 183.0 reduce-scatter.3
where the time goes:
time: 1480 us
  blocking collectives  880 us (59%)
  local copies, waits for them, and re-layouts  339 us (23%)
  waiting for transfers between devices  204 us (14%)
  starting transfers between devices  30.8 us (2%)
    all_gather x1, blocking collectives, shards(): lax.all_gather(faraway_part[0], 'seq', axis=0, tiled=True)  293 us
    all_gather x1, blocking collectives, shards(): lax.all_gather(faraway_part[1], 'seq', axis=0, tiled=True)  291 us
    all_gather x1, blocking collectives, shards(): lax.all_gather(faraway_part[2], 'seq', axis=0, tiled=True)  291 us
    unnamed x2, waiting for transfers between devices  183 us
    gather x8, local copies, waits for them, and re-layouts, select_rows(): jnp.take_along_axis(key_matrix.reshape(kept_rows, stride, heads_local, ke...  165 us
    gather x6, local copies, waits for them, and re-layouts, select_rows(): jnp.take_along_axis(value_matrix.reshape(kept_rows, stride, heads_local,...  164 us
  transfers between devices with their start and end apart: 20, of which 11 were waited for; matrix products, arithmetic and copies ran while one was open for 5% of the time, Pallas kernels for 0%

commit v1 on v0

v1 whole, which is shorter than its diff:
```python
import jax
import jax.numpy as jnp
from jax import lax
from jax.experimental import pallas as pl
from jax.experimental.pallas import tpu as pltpu
from jax.sharding import PartitionSpec as P

D = 768
HALF = 384
ROWS = 128
NX, NY, NZ = 4, 4, 8
SEG = 4
LONG = SEG * 8
NEG = -1e30
F32 = jnp.float32
BF16 = jnp.bfloat16
MESH = pl.DeviceIdType.MESH
PLAIN = (((1,), (0,)), ((), ()))
MINOR = (((1,), (1,)), ((), ()))
MAJOR = (((0,), (0,)), ((), ()))


def iota(shape, dim):
    return lax.broadcasted_iota(jnp.int32, shape, dim)


def dot(a, b, dims):
    return lax.dot_general(a, b, dims, preferred_element_type=F32)


def kernel(
    tiles, gain_in, w_qkv, w_out_in, src_in, cnt_in,
    out,
    w_v, w_out, gain, src, cnt, A, C, DD, E, SRC, R, PM, SEL,
    KS, VS, MKS, GF, HM, QA, M, L, O, AS, AT, PO, PI,
    w_sem, loc_sem,
    xs_s, xs_r, zs_s, zs_r, ps_s, ps_r, src_s, src_r,
    gf_s, gf_r, hm_s, hm_r, at_s, at_r, o_s, o_r,
):
    seq = lax.axis_index("seq")
    core = lax.axis_index("head")
    x, y, z = seq // (NY * NZ), (seq // NZ) % NY, seq % NZ
    zh, zj = z // SEG, z % SEG
    place = zj + zh * (SEG - 1 - 2 * zj)
    pair = (place + 1) // 2
    first_head = 6 * core + 2 * pair
    sibling = {"head": 1 - core}
    pending = []

    def at(px, py, pz):
        return {"seq": (px * NY + py) * NZ + pz}

    def remote(source, target, s_sem, r_sem, device):
        return pltpu.make_async_remote_copy(
            src_ref=source, dst_ref=target, send_sem=s_sem, recv_sem=r_sem,
            device_id=device, device_id_type=MESH,
        )

    def send(source, target, s_sem, r_sem, device):
        copy = remote(source, target, s_sem, r_sem, device)
        copy.start()
        pending.append(copy)
        return copy

    lanes = pl.ds(pl.multiple_of(pair * ROWS, ROWS), ROWS)
    weights = [
        pltpu.make_async_copy(w_qkv.at[t, :, lanes], w_v.at[:, t * ROWS : (t + 1) * ROWS], w_sem.at[t])
        for t in range(3)
    ]
    weights += [pltpu.make_async_copy(w_out_in, w_out, w_sem.at[3])]
    weights += [pltpu.make_async_copy(gain_in, gain, w_sem.at[4])]
    small = [
        pltpu.make_async_copy(src_in, src, loc_sem.at[1]),
        pltpu.make_async_copy(cnt_in, cnt, loc_sem.at[2]),
    ]
    own_a = pltpu.make_async_copy(tiles.at[x], A.at[0], loc_sem.at[0])
    barrier = pltpu.get_barrier_semaphore()
    peers = [at((x + k) % NX, y, z) for k in range(1, NX)] + [sibling]
    plane = [(o // NZ, o % NZ) for o in range(1, NY * NZ)]
    peers += [at(x, (y + dy) % NY, (z + dz) % NZ) for dy, dz in plane]
    for peer in peers:
        pl.semaphore_signal(barrier, inc=1, device_id=peer, device_id_type=MESH)
    for copy in small + weights + [own_a]:
        copy.start()
    for copy in small:
        copy.wait()
    own_count = cnt[0]
    rows8 = iota((8, ROWS), 0)
    tag = jnp.where(rows8 == 0, src[...] // ROWS, own_count)
    SRC[zj] = tag.astype(F32)
    pl.semaphore_wait(barrier, len(peers))

    in_x = [
        send(tiles.at[(x + k) % NX], A.at[k], xs_s.at[k], xs_r.at[k], at((x + k) % NX, y, z))
        for k in range(1, NX)
    ]
    in_src = [
        send(SRC.at[zj], SRC.at[zj], src_s.at[t], src_r.at[t], at(x, y, SEG * zh + (zj + t) % SEG))
        for t in range(1, SEG)
    ]
    own_a.wait()
    row, col = iota((ROWS, ROWS), 0), iota((ROWS, ROWS), 1)
    turn = (((row >> 2) & 3) * 32 + (row >> 4) * 4 + (row & 3) == col).astype(BF16)
    for copy in in_x:
        copy.wait_recv()
    turned = dot(turn, A[...].reshape(ROWS, HALF), PLAIN)
    C[...] = turned.astype(BF16).reshape(2 * NY, 16, HALF)

    in_z = [[] for _ in range(NY)]
    for dy, dz in plane:
        yt, zt = (y + dy) % NY, (z + dz) % NZ
        o = dy * NZ + dz
        in_z[dy].append(
            send(C.at[2 * yt + zt // SEG], DD.at[dy, dz], zs_s.at[o], zs_r.at[o], at(x, yt, zt))
        )
    DD[0, 0] = C[2 * y + zh]

    for copy in in_src:
        copy.wait_recv()
    lane512 = iota((1, 512), 1)
    from_x, from_y = (x + NX - ((lane512 >> 2) & 3)) & 3, (y + NY - (lane512 >> 7)) & 3
    from_z = (z + NZ - ((lane512 >> 4) & 7)) & 7
    code = (((from_x * NY + from_y) * NZ + from_z) * SEG + (lane512 & 3)).astype(F32)
    place_iota = iota((ROWS, ROWS), 0).astype(F32)
    for b in range(SEG):
        block = SRC[b]
        wanted = jnp.transpose(block)[:, 0:1] * SEG + b
        PM[b * ROWS : (b + 1) * ROWS] = (wanted == code).astype(BF16)
        alive = place_iota < block[1:2]
        MKS[b * ROWS : (b + 1) * ROWS] = jnp.where(alive, 0.0, NEG).astype(BF16)
        AS[b] = (iota((ROWS, ROWS), 1).astype(F32) < block[1:2]).astype(BF16)
        GF[0, 0, 0, 64 + b : 65 + b] = block[1:2].astype(BF16)
        QA[b, 0:ROWS, ROWS:] = (col == 0).astype(BF16)
        QA[b, ROWS:, ROWS:] = (col == 1).astype(BF16)
        M[b] = jnp.full((8, 256), NEG, F32)
        L[b] = jnp.zeros((8, 256), F32)
        O[b] = jnp.zeros((ROWS, 256), F32)
    GF[0, 0, 0, 68:72] = jnp.zeros((4, ROWS), BF16)
    out_row, from_row = iota((160, 512), 0), iota((160, 512), 1)
    for h in range(2):
        head = first_head + h
        mid = (out_row >> 5) * ROWS + (out_row & 31) * 4 + head % 4
        far_row = out_row - ROWS
        far = (far_row >> 3) * ROWS + (far_row & 7) * 16 + head
        SEL[h] = (jnp.where(out_row < ROWS, mid, far) == from_row).astype(BF16)
    for copy in weights:
        copy.wait()

    gain_mine = jnp.concatenate([gain[pl.ds(3 * core + i, 1)] for i in range(3)], axis=1)
    gain_other = jnp.concatenate([gain[pl.ds(3 - 3 * core + i, 1)] for i in range(3)], axis=1)
    w_mine = w_v[pl.ds(pl.multiple_of(core * HALF, HALF), HALF)]
    w_other = w_v[pl.ds(pl.multiple_of((1 - core) * HALF, HALF), HALF)]
    in_p = []

    def project(c):
        a = DD[c].reshape(ROWS, HALF).astype(F32)
        b = E[c].reshape(ROWS, HALF).astype(F32)
        mean = (jnp.sum(a, 1, keepdims=True) + jnp.sum(b, 1, keepdims=True)) / D
        a, b = a - mean, b - mean
        var = (jnp.sum(a * a, 1, keepdims=True) + jnp.sum(b * b, 1, keepdims=True)) / D
        scale = lax.rsqrt(var + 1e-05)
        a = (a * scale * gain_mine).astype(BF16)
        b = (b * scale * gain_other).astype(BF16)
        R[c * ROWS : (c + 1) * ROWS] = (dot(a, w_mine, PLAIN) + dot(b, w_other, PLAIN)).astype(BF16)

    for c in range(NY):
        for copy in in_z[c]:
            copy.wait_recv()
        in_p.append(send(DD.at[c], E.at[c], ps_s.at[c], ps_r.at[c], sibling))
        if c:
            in_p[c - 1].wait_recv()
            project(c - 1)
    in_p[NY - 1].wait_recv()
    project(NY - 1)

    qkv = dot(PM[...], R[...], PLAIN)
    kv = qkv[:, ROWS:].astype(BF16)
    low = (iota((1, 2 * ROWS), 1) & 127) < 64
    picked = jnp.where(low, dot(SEL[0], kv, PLAIN), dot(SEL[1], kv, PLAIN)).astype(BF16)
    HM[0, 0, 0:ROWS] = picked[0:ROWS, 0:ROWS]
    HM[0, 0, ROWS:] = picked[0:ROWS, ROWS:]
    GF[0, 0, 0, 0:LONG] = picked[ROWS:, 0:ROWS]
    GF[0, 0, 0, LONG : 2 * LONG] = picked[ROWS:, ROWS:]

    def z_of(f):
        return z + f * (NZ - 1 - 2 * z)

    y_pair = y + 1 - 2 * (y % 2)
    in_m = []
    for yy, f in ((1, 0), (0, 1), (1, 1)):
        in_m.append(
            send(
                HM.at[0, 0], HM.at[yy, f], hm_s.at[2 * yy + f], hm_r.at[2 * yy + f],
                at(x, y_pair if yy else y, z_of(f)),
            )
        )
    in_g = [[] for _ in range(NX)]
    for dx in (2, 1, 3, 0):
        for dy in (2, 1, 3, 0):
            for f in (1, 0):
                if dx or dy or f:
                    o = (dx * NY + dy) * 2 + f
                    in_g[dx].append(
                        send(
                            GF.at[0, 0, 0], GF.at[dx, dy, f], gf_s.at[o], gf_r.at[o],
                            at((x + dx) % NX, (y + dy) % NY, z_of(f)),
                        )
                    )
    KS[...] = kv[:, 0:ROWS]
    VS[...] = kv[:, ROWS:]
    q32 = qkv[:, 0:ROWS].astype(BF16).astype(F32) * 0.125
    for b in range(SEG):
        q_b = q32[b * ROWS : (b + 1) * ROWS]
        QA[b, 0:ROWS, 0:ROWS] = jnp.where(col < 64, q_b, 0.0).astype(BF16)
        QA[b, ROWS:, 0:ROWS] = jnp.where(col < 64, 0.0, q_b).astype(BF16)

    def absorb(keys, values, masks):
        keys = jnp.concatenate([keys, masks], axis=1)
        for b in range(SEG):
            scores = dot(keys, QA[b], MINOR)
            old = M[b][0:1]
            new = jnp.maximum(old, jnp.max(scores, axis=0, keepdims=True))
            weight = jnp.exp(scores - new)
            rescale = jnp.exp(old - new)
            total = L[b][0:1] * rescale + jnp.sum(weight, axis=0, keepdims=True)
            O[b] = O[b] * rescale + dot(values, weight.astype(BF16), MAJOR)
            M[b] = jnp.broadcast_to(new, (8, 256))
            L[b] = jnp.broadcast_to(total, (8, 256))

    def mask(n, counts, segment_rows, stride):
        r, c = iota((n, counts.shape[0]), 0), iota((n, counts.shape[0]), 1)
        per_block = segment_rows // SEG
        owner = ((r // segment_rows) * 8 + (r % segment_rows) // per_block == c).astype(BF16)
        position = (iota((n, ROWS), 0) % per_block) * stride
        position = position + (first_head + jnp.minimum(iota((n, ROWS), 1), 1)) % stride
        alive = position.astype(F32) < dot(owner, counts, PLAIN)
        return jnp.where(alive, 0.0, NEG).astype(BF16)

    absorb(KS[...], VS[...], MKS[...])

    for dx in (0, 1, 3, 2):
        for copy in in_g[dx]:
            copy.wait_recv()
        if dx == 0:
            for copy in in_m:
                copy.wait_recv()
            near = [GF[0, 0, 0, 64:72], GF[0, 0, 1, 64:72]]
            slot = NY - 1 - 2 * (y % 2)
            near += [GF[0, slot, 0, 64:72], GF[0, slot, 1, 64:72]]
            near = jnp.concatenate([part.astype(F32) for part in near], axis=0).astype(BF16)
            absorb(
                HM[:, :, 0:ROWS].reshape(512, ROWS),
                HM[:, :, ROWS:].reshape(512, ROWS),
                mask(512, near, ROWS, 4),
            )
        tags = GF[dx, :, :, 64:72].astype(F32).reshape(64, ROWS).astype(BF16)
        absorb(
            GF[dx, :, :, 0:LONG].reshape(256, ROWS),
            GF[dx, :, :, LONG : 2 * LONG].reshape(256, ROWS),
            mask(256, tags, LONG, 16),
        )

    for b in range(SEG):
        halves = []
        for h in range(2):
            cols = slice(h * ROWS, (h + 1) * ROWS)
            halves.append(O[b][h * 64 : (h + 1) * 64, cols] / L[b][0:1, cols])
        AS[b] = (jnp.concatenate(halves, axis=0) * AS[b].astype(F32)).astype(BF16)
    AT[pair] = AS[zj]
    backs = []
    for target in range(SEG):
        block = target + zh * (SEG - 1 - 2 * target)
        copy = remote(
            AS.at[block], AT.at[pair], at_s.at[target], at_r.at[pair], at(x, y, SEG * zh + block)
        )
        senders = [p for p in (0, 3) if p != target] + {0: [1], 3: [2]}.get(target, [])
        here = place == senders[0]
        for p in senders[1:]:
            here = here | (place == p)
        backs.append((copy, here))
        pl.when(here)(copy.start)
    for g in range(3):
        arrival = remote(AS.at[0], AT.at[g], at_s.at[0], at_r.at[g], sibling)
        pl.when(pair != g)(arrival.wait_recv)
    attended = AT[...].reshape(HALF, ROWS)
    mine = pl.ds(pl.multiple_of(core * HALF, HALF), HALF)
    other = pl.ds(pl.multiple_of((1 - core) * HALF, HALF), HALF)
    PO[...] = dot(attended, w_out[:, other], MAJOR).astype(BF16)
    in_o = send(PO, PI, o_s.at[0], o_r.at[0], sibling)
    own_part = dot(attended, w_out[:, mine], MAJOR)
    in_o.wait_recv()
    out[...] = (own_part + PI[...].astype(F32)).astype(BF16)
    for copy, here in backs:
        pl.when(here)(copy.wait_send)
    for copy in pending:
        copy.wait_send()


def shards(tiles, ln_gain, w_qkv, w_out, tile_source, tissue_count):
    dma = pltpu.SemaphoreType.DMA
    scratch = [
        pltpu.VMEM((D, 3 * ROWS), BF16),
        pltpu.VMEM((HALF, D), BF16),
        pltpu.VMEM((6, ROWS), F32),
        pltpu.VMEM((1, ROWS), jnp.int32),
        pltpu.SMEM((1,), jnp.int32),
        pltpu.VMEM((NX, 32, HALF), BF16),
        pltpu.VMEM((2 * NY, 16, HALF), BF16),
        pltpu.VMEM((NY, NZ, 16, HALF), BF16),
        pltpu.VMEM((NY, NZ, 16, HALF), BF16),
        pltpu.VMEM((SEG, 8, ROWS), F32),
        pltpu.VMEM((512, 3 * ROWS), BF16),
        pltpu.VMEM((512, 512), BF16),
        pltpu.VMEM((2, 160, 512), BF16),
        pltpu.VMEM((512, ROWS), BF16),
        pltpu.VMEM((512, ROWS), BF16),
        pltpu.VMEM((512, ROWS), BF16),
        pltpu.VMEM((NX, NY, 2, 72, ROWS), BF16),
        pltpu.VMEM((2, 2, 256, ROWS), BF16),
        pltpu.VMEM((SEG, 256, 256), BF16),
        pltpu.VMEM((SEG, 8, 256), F32),
        pltpu.VMEM((SEG, 8, 256), F32),
        pltpu.VMEM((SEG, ROWS, 256), F32),
        pltpu.VMEM((SEG, ROWS, ROWS), BF16),
        pltpu.VMEM((3, ROWS, ROWS), BF16),
        pltpu.VMEM((ROWS, HALF), BF16),
        pltpu.VMEM((ROWS, HALF), BF16),
        dma((5,)), dma((3,)),
    ]
    for size in (NX, NY * NZ, NY, SEG, NX * NY * 2, 4, SEG, 1):
        scratch += [dma((size,)), dma((size,))]
    anywhere = pl.BlockSpec(memory_space=pl.ANY)
    return pl.pallas_call(
        kernel,
        out_shape=jax.ShapeDtypeStruct((ROWS, HALF), BF16),
        in_specs=[anywhere] * 6,
        out_specs=pl.BlockSpec(memory_space=pltpu.VMEM),
        scratch_shapes=scratch,
        compiler_params=pltpu.CompilerParams(
            collective_id=0, has_side_effects=True, vmem_limit_bytes=48 << 20
        ),
    )(
        tiles.reshape(NX, 32, HALF),
        ln_gain.reshape(6, ROWS),
        jnp.transpose(w_qkv, (1, 0, 2)),
        w_out,
        tile_source.reshape(1, ROWS),
        tissue_count,
    )


def solution(mesh):
    return jax.shard_map(
        shards,
        mesh=mesh,
        in_specs=(
            P("seq", "head"),
            P(),
            P(None, None, "head"),
            P("head", None),
            P("seq"),
            P("seq"),
        ),
        out_specs=P("seq", "head"),
        check_vma=False,
    )
```

time: 1480 us -> 70.6 us (0.05)
  blocking collectives: 880 us -> 0 us
  local copies, waits for them, and re-layouts: 339 us -> 5.41 us
  waiting for transfers between devices: 204 us -> 0 us
  Pallas kernels: 0 us -> 64.3 us
  starting transfers between devices: 30.8 us -> 0 us
    all_gather x4 -> x0, blocking collectives: 880 us -> none  [the longest x1 293 us: shards(): lax.all_gather(faraway_part[0], 'seq', axis=0, tiled=True)]
    gather x18 -> x0, local copies, waits for them, and re-layouts: 331 us -> none  [the longest x8 165 us: select_rows(): jnp.take_along_axis(key_matrix.reshape(kept_rows, stride, heads_local, ke...]
    unnamed x2 -> x0, waiting for transfers between devices: 183 us -> none
    pallas_call x0 -> x1, Pallas kernels: none -> 64.3 us  [shards(): pl.pallas_call(kernel, out_shape=jax.ShapeDtypeStruct((ROWS, HALF), BF16)...]
    ppermute x18 -> x0, waiting for transfers between devices: 21.2 us -> none  [swapped(): lax.ppermute(value, axis, [(i, i ^ 1 << apart) for i in range(lax.axis_si...]
    ppermute x18 -> x0, starting transfers between devices: 17 us -> none  [swapped(): lax.ppermute(value, axis, [(i, i ^ 1 << apart) for i in range(lax.axis_si...]
  transfers between devices with their start and end apart: 20 -> 0, of which waited for: 11 -> 0; matrix products, arithmetic and copies ran while one was open for 5% -> 0% of each run, Pallas kernels for 0% -> 0%
where the time goes in v1:
time: 70.6 us; the launch traced here: 70.4 us
  Pallas kernels  64.3 us (91%)
  local copies, waits for them, and re-layouts  5.41 us (8%)
    pallas_call x1, Pallas kernels, shards(): pl.pallas_call(kernel, out_shape=jax.ShapeDtypeStruct((ROWS, HALF), BF16)...  64.3 us
    unnamed x11, local copies, waits for them, and re-layouts  5.41 us

profile of v1, /device:TPU:1, one launch (start us, length us, event | category | flops | bytes accessed | tf_op | source)
XLA Modules:
  0.0 70.4 jit_solution(2186581044691814407)
XLA Ops:
  0.7 0.0 copy-start
  0.7 1.5 %copy-done = bf16[768,3,384]{2,0,1:T(8,128)(2,1)S(1)} copy-done((bf16[768,3,384]{2,0,1:T(8,128)(2,1)S(1)}, bf16[768,3,384]{2,0,1:T(8,128)(2,1)}, u32[]{:S(2)}) %copy-start) | copy-done | bytes 1769496
  2.1 0.0 copy-start.1
  2.1 1.1 %copy-done.1 = bf16[384,768]{1,0:T(8,128)(2,1)S(1)} copy-done((bf16[384,768]{1,0:T(8,128)(2,1)S(1)}, bf16[384,768]{1,0:T(8,128)(2,1)}, u32[]{:S(2)}) %copy-start.1) | copy-done | bytes 589848
  3.2 0.0 copy-start.2
  3.2 0.9 %copy-done.2 = bf16[128,384]{1,0:T(8,128)(2,1)S(1)} copy-done((bf16[128,384]{1,0:T(8,128)(2,1)S(1)}, bf16[128,384]{1,0:T(8,128)(2,1)}, u32[]{:S(2)}) %copy-start.2) | copy-done | bytes 98328
  4.1 0.0 copy-start.3
  4.1 0.7 copy-done.3
  4.8 0.0 copy-start.4
  4.8 0.7 copy-done.4
  5.4 64.3 %shard_map.64 = bf16[128,384]{1,0:T(8,128)(2,1)S(1)} custom-call(bf16[4,32,384]{2,1,0:T(8,128)(2,1)S(1)} %bitcast.5, f32[6,128]{1,0:T(8,128)S(1)} %bitcast.6, bf16[3,768,384]{2,1,0:T(8,128)(2,1)S(1)} %bitcast.4, bf16[384,768]{1,0:T(8,128)(2,1)S(1)} %copy-done.1, s32[1,128]{1,0:T(1,128)S(1)} %bitcast.7, s32[1]{0:T(128)S(6)} %copy.8.cnt_in), custom_call_target="tpu_custom_call" | custom-call | tf_op jit(solution)/shard_map/pallas_call | solution.py:333
  69.8 0.6 copy.9
Async XLA Ops:
  0.7 1.5 %copy-start = (bf16[768,3,384]{2,0,1:T(8,128)(2,1)S(1)}, bf16[768,3,384]{2,0,1:T(8,128)(2,1)}, u32[]{:S(2)}) copy-start(bf16[768,3,384]{2,0,1:T(8,128)(2,1)} %param.8) | copy-start | bytes 5308420
  2.1 1.1 %copy-start.1 = (bf16[384,768]{1,0:T(8,128)(2,1)S(1)}, bf16[384,768]{1,0:T(8,128)(2,1)}, u32[]{:S(2)}) copy-start(bf16[384,768]{1,0:T(8,128)(2,1)} %w_out_in.1) | copy-start | bytes 1769476
  3.2 0.9 %copy-start.2 = (bf16[128,384]{1,0:T(8,128)(2,1)S(1)}, bf16[128,384]{1,0:T(8,128)(2,1)}, u32[]{:S(2)}) copy-start(bf16[128,384]{1,0:T(8,128)(2,1)} %param.6) | copy-start | bytes 294916
  4.1 0.7 copy-start.3
  4.8 0.7 copy-start.4

commit v2 on v1

--- a/solution.py
+++ b/solution.py
@@ -31,7 +31,7 @@
 def kernel(
     tiles, gain_in, w_qkv, w_out_in, src_in, cnt_in,
     out,
-    w_v, w_out, gain, src, cnt, A, C, DD, E, SRC, R, PM, SEL,
+    w_v, w_out, gain, src, cnt, T, A, C, DD, E, SRC, R, PM, SEL,
     KS, VS, MKS, GF, HM, QA, M, L, O, AS, AT, PO, PI,
     w_sem, loc_sem,
     xs_s, xs_r, zs_s, zs_r, ps_s, ps_r, src_s, src_r,
@@ -73,16 +73,16 @@
         pltpu.make_async_copy(src_in, src, loc_sem.at[1]),
         pltpu.make_async_copy(cnt_in, cnt, loc_sem.at[2]),
     ]
-    own_a = pltpu.make_async_copy(tiles.at[x], A.at[0], loc_sem.at[0])
+    own_t = pltpu.make_async_copy(tiles, T, loc_sem.at[0])
     barrier = pltpu.get_barrier_semaphore()
     peers = [at((x + k) % NX, y, z) for k in range(1, NX)] + [sibling]
     plane = [(o // NZ, o % NZ) for o in range(1, NY * NZ)]
     peers += [at(x, (y + dy) % NY, (z + dz) % NZ) for dy, dz in plane]
     for peer in peers:
         pl.semaphore_signal(barrier, inc=1, device_id=peer, device_id_type=MESH)
-    for copy in small + weights + [own_a]:
+    for copy in small + [own_t] + weights:
         copy.start()
-    for copy in small:
+    for copy in small + [own_t]:
         copy.wait()
     own_count = cnt[0]
     rows8 = iota((8, ROWS), 0)
@@ -91,14 +91,14 @@
     pl.semaphore_wait(barrier, len(peers))
 
     in_x = [
-        send(tiles.at[(x + k) % NX], A.at[k], xs_s.at[k], xs_r.at[k], at((x + k) % NX, y, z))
+        send(T.at[(x + k) % NX], A.at[k], xs_s.at[k], xs_r.at[k], at((x + k) % NX, y, z))
         for k in range(1, NX)
     ]
     in_src = [
         send(SRC.at[zj], SRC.at[zj], src_s.at[t], src_r.at[t], at(x, y, SEG * zh + (zj + t) % SEG))
         for t in range(1, SEG)
     ]
-    own_a.wait()
+    A[0] = T[x]
     row, col = iota((ROWS, ROWS), 0), iota((ROWS, ROWS), 1)
     turn = (((row >> 2) & 3) * 32 + (row >> 4) * 4 + (row & 3) == col).astype(BF16)
     for copy in in_x:
@@ -182,30 +182,23 @@
     GF[0, 0, 0, 0:LONG] = picked[ROWS:, 0:ROWS]
     GF[0, 0, 0, LONG : 2 * LONG] = picked[ROWS:, ROWS:]
 
-    def z_of(f):
-        return z + f * (NZ - 1 - 2 * z)
-
-    y_pair = y + 1 - 2 * (y % 2)
-    in_m = []
-    for yy, f in ((1, 0), (0, 1), (1, 1)):
-        in_m.append(
-            send(
-                HM.at[0, 0], HM.at[yy, f], hm_s.at[2 * yy + f], hm_r.at[2 * yy + f],
-                at(x, y_pair if yy else y, z_of(f)),
-            )
+    def to_xy(f, o):
+        dx, dy = o // NY, o % NY
+        return send(
+            GF.at[0, 0, f], GF.at[dx, dy, f], gf_s.at[2 * o + f], gf_r.at[2 * o + f],
+            at((x + dx) % NX, (y + dy) % NY, z),
         )
-    in_g = [[] for _ in range(NX)]
-    for dx in (2, 1, 3, 0):
-        for dy in (2, 1, 3, 0):
-            for f in (1, 0):
-                if dx or dy or f:
-                    o = (dx * NY + dy) * 2 + f
-                    in_g[dx].append(
-                        send(
-                            GF.at[0, 0, 0], GF.at[dx, dy, f], gf_s.at[o], gf_r.at[o],
-                            at((x + dx) % NX, (y + dy) % NY, z_of(f)),
-                        )
-                    )
+
+    def middle(yy, f, source, device):
+        o = 2 * yy + f
+        return send(source, HM.at[yy, f], hm_s.at[o], hm_r.at[o], device)
+
+    mirror, partner = at(x, y, NZ - 1 - z), at(x, y + 1 - 2 * (y % 2), z)
+    order = (10, 11, 9, 14, 6, 2, 8, 3, 1, 12, 4, 7, 13, 15, 5)
+    in_far = send(GF.at[0, 0, 0], GF.at[0, 0, 1], gf_s.at[1], gf_r.at[1], mirror)
+    in_m01 = middle(0, 1, HM.at[0, 0], mirror)
+    in_near = {o: to_xy(0, o) for o in order}
+    in_m10 = middle(1, 0, HM.at[0, 0], partner)
     KS[...] = kv[:, 0:ROWS]
     VS[...] = kv[:, ROWS:]
     q32 = qkv[:, 0:ROWS].astype(BF16).astype(F32) * 0.125
@@ -214,7 +207,7 @@
         QA[b, 0:ROWS, 0:ROWS] = jnp.where(col < 64, q_b, 0.0).astype(BF16)
         QA[b, ROWS:, 0:ROWS] = jnp.where(col < 64, 0.0, q_b).astype(BF16)
 
-    def absorb(keys, values, masks):
+    def absorb(keys, values, masks, finish=None):
         keys = jnp.concatenate([keys, masks], axis=1)
         for b in range(SEG):
             scores = dot(keys, QA[b], MINOR)
@@ -226,6 +219,8 @@
             O[b] = O[b] * rescale + dot(values, weight.astype(BF16), MAJOR)
             M[b] = jnp.broadcast_to(new, (8, 256))
             L[b] = jnp.broadcast_to(total, (8, 256))
+            if finish is not None:
+                finish(b)
 
     def mask(n, counts, segment_rows, stride):
         r, c = iota((n, counts.shape[0]), 0), iota((n, counts.shape[0]), 1)
@@ -236,49 +231,61 @@
         alive = position.astype(F32) < dot(owner, counts, PLAIN)
         return jnp.where(alive, 0.0, NEG).astype(BF16)
 
+    in_far.wait_recv()
+    in_other = {o: to_xy(1, o) for o in order}
     absorb(KS[...], VS[...], MKS[...])
-
-    for dx in (0, 1, 3, 2):
-        for copy in in_g[dx]:
-            copy.wait_recv()
-        if dx == 0:
-            for copy in in_m:
-                copy.wait_recv()
-            near = [GF[0, 0, 0, 64:72], GF[0, 0, 1, 64:72]]
-            slot = NY - 1 - 2 * (y % 2)
-            near += [GF[0, slot, 0, 64:72], GF[0, slot, 1, 64:72]]
-            near = jnp.concatenate([part.astype(F32) for part in near], axis=0).astype(BF16)
-            absorb(
-                HM[:, :, 0:ROWS].reshape(512, ROWS),
-                HM[:, :, ROWS:].reshape(512, ROWS),
-                mask(512, near, ROWS, 4),
-            )
-        tags = GF[dx, :, :, 64:72].astype(F32).reshape(64, ROWS).astype(BF16)
+    in_m01.wait_recv()
+    in_m11 = middle(1, 1, HM.at[0, 1], partner)
+
+    def whole(dx, f, finish=None):
+        tags = GF[dx : dx + 2, :, f, 64:72].astype(F32).reshape(64, ROWS).astype(BF16)
         absorb(
-            GF[dx, :, :, 0:LONG].reshape(256, ROWS),
-            GF[dx, :, :, LONG : 2 * LONG].reshape(256, ROWS),
+            GF[dx : dx + 2, :, f, 0:LONG].reshape(256, ROWS),
+            GF[dx : dx + 2, :, f, LONG : 2 * LONG].reshape(256, ROWS),
             mask(256, tags, LONG, 16),
+            finish,
         )
 
-    for b in range(SEG):
+    for dx in (0, 2):
+        for o in order:
+            if o // NY in (dx, dx + 1):
+                in_near[o].wait_recv()
+        whole(dx, 0)
+    in_other[1].wait_recv()
+    in_other[3].wait_recv()
+    in_m10.wait_recv()
+    in_m11.wait_recv()
+    tags = [GF[0, 0, 0, 64:72], GF[0, 0, 1, 64:72]]
+    slot = NY - 1 - 2 * (y % 2)
+    tags += [GF[0, slot, 0, 64:72], GF[0, slot, 1, 64:72]]
+    tags = jnp.concatenate([part.astype(F32) for part in tags], axis=0).astype(BF16)
+    absorb(
+        HM[:, :, 0:ROWS].reshape(512, ROWS),
+        HM[:, :, ROWS:].reshape(512, ROWS),
+        mask(512, tags, ROWS, 4),
+    )
+    backs = []
+
+    def give_back(b):
         halves = []
         for h in range(2):
             cols = slice(h * ROWS, (h + 1) * ROWS)
             halves.append(O[b][h * 64 : (h + 1) * 64, cols] / L[b][0:1, cols])
         AS[b] = (jnp.concatenate(halves, axis=0) * AS[b].astype(F32)).astype(BF16)
-    AT[pair] = AS[zj]
-    backs = []
-    for target in range(SEG):
-        block = target + zh * (SEG - 1 - 2 * target)
-        copy = remote(
-            AS.at[block], AT.at[pair], at_s.at[target], at_r.at[pair], at(x, y, SEG * zh + block)
-        )
-        senders = [p for p in (0, 3) if p != target] + {0: [1], 3: [2]}.get(target, [])
-        here = place == senders[0]
-        for p in senders[1:]:
-            here = here | (place == p)
+        target = b + zh * (SEG - 1 - 2 * b)
+        here = (place == 0) | (place == 3)
+        here = here | ((place == 1) & (target == 0)) | ((place == 2) & (target == 3))
+        here = here & (place != target)
+        copy = remote(AS.at[b], AT.at[pair], at_s.at[b], at_r.at[pair], at(x, y, SEG * zh + b))
         backs.append((copy, here))
         pl.when(here)(copy.start)
+
+    for dx in (0, 2):
+        for o in order:
+            if o // NY in (dx, dx + 1) and o not in (1, 3):
+                in_other[o].wait_recv()
+        whole(dx, 1, give_back if dx else None)
+    AT[pair] = AS[zj]
     for g in range(3):
         arrival = remote(AS.at[0], AT.at[g], at_s.at[0], at_r.at[g], sibling)
         pl.when(pair != g)(arrival.wait_recv)
@@ -304,6 +311,7 @@
         pltpu.VMEM((6, ROWS), F32),
         pltpu.VMEM((1, ROWS), jnp.int32),
         pltpu.SMEM((1,), jnp.int32),
+        pltpu.VMEM((NX, 32, HALF), BF16),
         pltpu.VMEM((NX, 32, HALF), BF16),
         pltpu.VMEM((2 * NY, 16, HALF), BF16),
         pltpu.VMEM((NY, NZ, 16, HALF), BF16),
@@ -329,7 +337,7 @@
     ]
     for size in (NX, NY * NZ, NY, SEG, NX * NY * 2, 4, SEG, 1):
         scratch += [dma((size,)), dma((size,))]
-    anywhere = pl.BlockSpec(memory_space=pl.ANY)
+    anywhere = pl.BlockSpec(memory_space=pltpu.HBM)
     return pl.pallas_call(
         kernel,
         out_shape=jax.ShapeDtypeStruct((ROWS, HALF), BF16),
@@ -337,7 +345,7 @@
         out_specs=pl.BlockSpec(memory_space=pltpu.VMEM),
         scratch_shapes=scratch,
         compiler_params=pltpu.CompilerParams(
-            collective_id=0, has_side_effects=True, vmem_limit_bytes=48 << 20
+            collective_id=0, has_side_effects=True, vmem_limit_bytes=64 << 20
         ),
     )(
         tiles.reshape(NX, 32, HALF),

time: 70.6 us -> 53.8 us (0.76)
  Pallas kernels: 64.3 us -> 51.5 us
  local copies, waits for them, and re-layouts: 5.41 us -> 1.54 us
    pallas_call x1, Pallas kernels: 64.3 us -> 51.5 us  [shards(): pl.pallas_call(kernel, out_shape=jax.ShapeDtypeStruct((ROWS, HALF), BF16)...]
    unnamed x11 -> x1, local copies, waits for them, and re-layouts: 5.41 us -> 1.54 us
where the time goes in v2:
time: 53.8 us; the launch traced here: 53.7 us
  Pallas kernels  51.5 us (96%)
  local copies, waits for them, and re-layouts  1.54 us (3%)
  between operations  0.66 us (1%)
    pallas_call x1, Pallas kernels, shards(): pl.pallas_call(kernel, out_shape=jax.ShapeDtypeStruct((ROWS, HALF), BF16)...  51.5 us
    unnamed x1, local copies, waits for them, and re-layouts  1.54 us

profile of v2, /device:TPU:1, one launch (start us, length us, event | category | flops | bytes accessed | tf_op | source)
XLA Modules:
  0.0 53.7 jit_solution(8981938952761562164)
XLA Ops:
  0.7 51.5 %shard_map.64 = bf16[128,384]{1,0:T(8,128)(2,1)} custom-call(bf16[4,32,384]{2,1,0:T(8,128)(2,1)} %bitcast.5, f32[6,128]{1,0:T(8,128)} %bitcast.6, bf16[3,768,384]{2,1,0:T(8,128)(2,1)} %bitcast.4, bf16[384,768]{1,0:T(8,128)(2,1)} %w_out_in.1, s32[1,128]{1,0:T(1,128)} %bitcast.7, s32[1]{0:T(128)S(6)} %copy.8.cnt_in), custom_call_target="tpu_custom_call" | custom-call | tf_op jit(solution)/shard_map/pallas_call | solution.py:341
  52.1 1.5 %copy.9 = bf16[128,384]{1,0:T(8,128)(2,1)} copy(bf16[128,384]{1,0:T(8,128)(2,1)} %shard_map.64) | data formatting | bytes 196608

commit v3 on v2

--- a/solution.py
+++ b/solution.py
@@ -30,10 +30,10 @@
 
 def kernel(
     tiles, gain_in, w_qkv, w_out_in, src_in, cnt_in,
-    out,
+    own_part, other_part,
     w_v, w_out, gain, src, cnt, T, A, C, DD, E, SRC, R, PM, SEL,
-    KS, VS, MKS, GF, HM, QA, M, L, O, AS, AT, PO, PI,
-    w_sem, loc_sem,
+    KS, VS, MKS, GF, HM, QA, M, L, O, AS, AT, PO, OWN,
+    w_sem, loc_sem, ready,
     xs_s, xs_r, zs_s, zs_r, ps_s, ps_r, src_s, src_r,
     gf_s, gf_r, hm_s, hm_r, at_s, at_r, o_s, o_r,
 ):
@@ -42,7 +42,7 @@
     x, y, z = seq // (NY * NZ), (seq // NZ) % NY, seq % NZ
     zh, zj = z // SEG, z % SEG
     place = zj + zh * (SEG - 1 - 2 * zj)
-    pair = (place + 1) // 2
+    pair = place % 3
     first_head = 6 * core + 2 * pair
     sibling = {"head": 1 - core}
     pending = []
@@ -77,7 +77,8 @@
     barrier = pltpu.get_barrier_semaphore()
     peers = [at((x + k) % NX, y, z) for k in range(1, NX)] + [sibling]
     plane = [(o // NZ, o % NZ) for o in range(1, NY * NZ)]
-    peers += [at(x, (y + dy) % NY, (z + dz) % NZ) for dy, dz in plane]
+    y_peers = [at(x, (y + k) % NY, z) for k in range(1, NY)]
+    peers += y_peers + [at(x, y, (z + k) % NZ) for k in range(1, NZ)]
     for peer in peers:
         pl.semaphore_signal(barrier, inc=1, device_id=peer, device_id_type=MESH)
     for copy in small + [own_t] + weights:
@@ -89,6 +90,8 @@
     tag = jnp.where(rows8 == 0, src[...] // ROWS, own_count)
     SRC[zj] = tag.astype(F32)
     pl.semaphore_wait(barrier, len(peers))
+    for peer in y_peers:
+        pl.semaphore_signal(ready, inc=1, device_id=peer, device_id_type=MESH)
 
     in_x = [
         send(T.at[(x + k) % NX], A.at[k], xs_s.at[k], xs_r.at[k], at((x + k) % NX, y, z))
@@ -103,6 +106,7 @@
     turn = (((row >> 2) & 3) * 32 + (row >> 4) * 4 + (row & 3) == col).astype(BF16)
     for copy in in_x:
         copy.wait_recv()
+    pl.semaphore_wait(ready, len(y_peers))
     turned = dot(turn, A[...].reshape(ROWS, HALF), PLAIN)
     C[...] = turned.astype(BF16).reshape(2 * NY, 16, HALF)
 
@@ -209,15 +213,18 @@
 
     def absorb(keys, values, masks, finish=None):
         keys = jnp.concatenate([keys, masks], axis=1)
-        for b in range(SEG):
-            scores = dot(keys, QA[b], MINOR)
-            old = M[b][0:1]
-            new = jnp.maximum(old, jnp.max(scores, axis=0, keepdims=True))
-            weight = jnp.exp(scores - new)
-            rescale = jnp.exp(old - new)
-            total = L[b][0:1] * rescale + jnp.sum(weight, axis=0, keepdims=True)
-            O[b] = O[b] * rescale + dot(values, weight.astype(BF16), MAJOR)
-            M[b] = jnp.broadcast_to(new, (8, 256))
+        turned_values = jnp.transpose(values)
+        blocks = range(SEG)
+        scores = [dot(keys, QA[b], MINOR) for b in blocks]
+        old = [M[b][0:1] for b in blocks]
+        new = [jnp.maximum(old[b], jnp.max(scores[b], axis=0, keepdims=True)) for b in blocks]
+        weight = [jnp.exp(scores[b] - new[b]) for b in blocks]
+        rescale = [jnp.exp(old[b] - new[b]) for b in blocks]
+        mixed = [dot(turned_values, weight[b].astype(BF16), PLAIN) for b in blocks]
+        for b in blocks:
+            total = L[b][0:1] * rescale[b] + jnp.sum(weight[b], axis=0, keepdims=True)
+            O[b] = O[b] * rescale[b] + mixed[b]
+            M[b] = jnp.broadcast_to(new[b], (8, 256))
             L[b] = jnp.broadcast_to(total, (8, 256))
             if finish is not None:
                 finish(b)
@@ -231,9 +238,9 @@
         alive = position.astype(F32) < dot(owner, counts, PLAIN)
         return jnp.where(alive, 0.0, NEG).astype(BF16)
 
+    absorb(KS[...], VS[...], MKS[...])
     in_far.wait_recv()
     in_other = {o: to_xy(1, o) for o in order}
-    absorb(KS[...], VS[...], MKS[...])
     in_m01.wait_recv()
     in_m11 = middle(1, 1, HM.at[0, 1], partner)
 
@@ -273,8 +280,8 @@
             halves.append(O[b][h * 64 : (h + 1) * 64, cols] / L[b][0:1, cols])
         AS[b] = (jnp.concatenate(halves, axis=0) * AS[b].astype(F32)).astype(BF16)
         target = b + zh * (SEG - 1 - 2 * b)
-        here = (place == 0) | (place == 3)
-        here = here | ((place == 1) & (target == 0)) | ((place == 2) & (target == 3))
+        here = (place == 1) | (place == 2)
+        here = here | ((place == 0) & (target == 1)) | ((place == 3) & (target == 2))
         here = here & (place != target)
         copy = remote(AS.at[b], AT.at[pair], at_s.at[b], at_r.at[pair], at(x, y, SEG * zh + b))
         backs.append((copy, here))
@@ -293,10 +300,12 @@
     mine = pl.ds(pl.multiple_of(core * HALF, HALF), HALF)
     other = pl.ds(pl.multiple_of((1 - core) * HALF, HALF), HALF)
     PO[...] = dot(attended, w_out[:, other], MAJOR).astype(BF16)
-    in_o = send(PO, PI, o_s.at[0], o_r.at[0], sibling)
-    own_part = dot(attended, w_out[:, mine], MAJOR)
+    in_o = send(PO, other_part, o_s.at[0], o_r.at[0], sibling)
+    OWN[...] = dot(attended, w_out[:, mine], MAJOR)
+    hand_out = pltpu.make_async_copy(OWN, own_part, loc_sem.at[0])
+    hand_out.start()
+    hand_out.wait()
     in_o.wait_recv()
-    out[...] = (own_part + PI[...].astype(F32)).astype(BF16)
     for copy, here in backs:
         pl.when(here)(copy.wait_send)
     for copy in pending:
@@ -332,17 +341,20 @@
         pltpu.VMEM((SEG, ROWS, ROWS), BF16),
         pltpu.VMEM((3, ROWS, ROWS), BF16),
         pltpu.VMEM((ROWS, HALF), BF16),
-        pltpu.VMEM((ROWS, HALF), BF16),
-        dma((5,)), dma((3,)),
+        pltpu.VMEM((ROWS, HALF), F32),
+        dma((5,)), dma((3,)), pltpu.SemaphoreType.REGULAR,
     ]
     for size in (NX, NY * NZ, NY, SEG, NX * NY * 2, 4, SEG, 1):
         scratch += [dma((size,)), dma((size,))]
     anywhere = pl.BlockSpec(memory_space=pltpu.HBM)
-    return pl.pallas_call(
+    own_part, other_part = pl.pallas_call(
         kernel,
-        out_shape=jax.ShapeDtypeStruct((ROWS, HALF), BF16),
+        out_shape=(
+            jax.ShapeDtypeStruct((ROWS, HALF), F32),
+            jax.ShapeDtypeStruct((ROWS, HALF), BF16),
+        ),
         in_specs=[anywhere] * 6,
-        out_specs=pl.BlockSpec(memory_space=pltpu.VMEM),
+        out_specs=(anywhere, anywhere),
         scratch_shapes=scratch,
         compiler_params=pltpu.CompilerParams(
             collective_id=0, has_side_effects=True, vmem_limit_bytes=64 << 20
@@ -355,6 +367,7 @@
         tile_source.reshape(1, ROWS),
         tissue_count,
     )
+    return (own_part + other_part.astype(F32)).astype(BF16)
 
 
 def solution(mesh):

time: 53.8 us -> 50.4 us (0.937)
  Pallas kernels: 51.5 us -> 47.9 us
  other arithmetic: 0 us -> 1.65 us
  local copies, waits for them, and re-layouts: 1.54 us -> 0 us
    pallas_call x1, Pallas kernels: 51.5 us -> 47.9 us  [shards(): pl.pallas_call(kernel, out_shape=(jax.ShapeDtypeStruct((ROWS, HALF), F32)...]
    convert_element_type x0 -> x1, other arithmetic: none -> 1.65 us  [shards(): return (own_part + other_part.astype(F32)).astype(BF16)]
    unnamed x1 -> x0, local copies, waits for them, and re-layouts: 1.54 us -> none
where the time goes in v3:
time: 50.4 us; the launch traced here: 50.2 us
  Pallas kernels  47.9 us (95%)
  other arithmetic  1.65 us (3%)
  between operations  0.66 us (1%)
    pallas_call x1, Pallas kernels, shards(): pl.pallas_call(kernel, out_shape=(jax.ShapeDtypeStruct((ROWS, HALF), F32)...  47.9 us
    convert_element_type x1, other arithmetic, shards(): return (own_part + other_part.astype(F32)).astype(BF16)  1.65 us

profile of v3, /device:TPU:1, one launch (start us, length us, event | category | flops | bytes accessed | tf_op | source)
XLA Modules:
  0.0 50.2 jit_solution(15935407378542647619)
XLA Ops:
  0.7 47.9 %shard_map.64 = (f32[128,384]{1,0:T(8,128)}, bf16[128,384]{1,0:T(8,128)(2,1)}) custom-call(bf16[4,32,384]{2,1,0:T(8,128)(2,1)} %bitcast.5, f32[6,128]{1,0:T(8,128)} %bitcast.6, bf16[3,768,384]{2,1,0:T(8,128)(2,1)} %bitcast.4, bf16[384,768]{1,0:T(8,128)(2,1)} %w_out_in.1, s32[1,128]{1,0:T(1,128)} %bitcast.7, s32[1]{0:T(128)S(6)} %copy.7.cnt_in), custom_call_target="tpu_custom_call" | custom-call | tf_op jit(solution)/shard_map/pallas_call | solution.py:350
  48.6 1.7 %add_convert_fusion = bf16[128,384]{1,0:T(8,128)(2,1)} fusion(f32[128,384]{1,0:T(8,128)} %get-tuple-element.7, bf16[128,384]{1,0:T(8,128)(2,1)} %get-tuple-element.8), kind=kLoop, calls=%fused_computation | loop fusion | flops 147456 | bytes 393216 | tf_op jit(solution)/shard_map/convert_element_type | solution.py:370

commit v4 on v3

--- a/solution.py
+++ b/solution.py
@@ -32,10 +32,11 @@
     tiles, gain_in, w_qkv, w_out_in, src_in, cnt_in,
     own_part, other_part,
     w_v, w_out, gain, src, cnt, T, A, C, DD, E, SRC, R, PM, SEL,
-    KS, VS, MKS, GF, HM, QA, M, L, O, AS, AT, PO, OWN,
+    KS, VS, MKS, MKM, MKL, CX, CY, CZ, GF, HM, QA, M, L, O, AS, AT, PO, OWN,
     w_sem, loc_sem, ready,
     xs_s, xs_r, zs_s, zs_r, ps_s, ps_r, src_s, src_r,
     gf_s, gf_r, hm_s, hm_r, at_s, at_r, o_s, o_r,
+    cx_s, cx_r, cy_s, cy_r, cz_s, cz_r,
 ):
     seq = lax.axis_index("seq")
     core = lax.axis_index("head")
@@ -89,12 +90,17 @@
     rows8 = iota((8, ROWS), 0)
     tag = jnp.where(rows8 == 0, src[...] // ROWS, own_count)
     SRC[zj] = tag.astype(F32)
+    CX[0] = jnp.where(iota((8, ROWS), 1) == seq, own_count, 0).astype(F32)
     pl.semaphore_wait(barrier, len(peers))
     for peer in y_peers:
         pl.semaphore_signal(ready, inc=1, device_id=peer, device_id_type=MESH)
 
     in_x = [
         send(T.at[(x + k) % NX], A.at[k], xs_s.at[k], xs_r.at[k], at((x + k) % NX, y, z))
+        for k in range(1, NX)
+    ]
+    in_cx = [
+        send(CX.at[0], CX.at[k], cx_s.at[k], cx_r.at[k], at((x + k) % NX, y, z))
         for k in range(1, NX)
     ]
     in_src = [
@@ -118,6 +124,10 @@
             send(C.at[2 * yt + zt // SEG], DD.at[dy, dz], zs_s.at[o], zs_r.at[o], at(x, yt, zt))
         )
     DD[0, 0] = C[2 * y + zh]
+    for copy in in_cx:
+        copy.wait_recv()
+    CY[0] = jnp.sum(CX[...], axis=0)
+    in_cy = [send(CY.at[0], CY.at[k], cy_s.at[k], cy_r.at[k], y_peers[k - 1]) for k in range(1, NY)]
 
     for copy in in_src:
         copy.wait_recv()
@@ -133,20 +143,26 @@
         alive = place_iota < block[1:2]
         MKS[b * ROWS : (b + 1) * ROWS] = jnp.where(alive, 0.0, NEG).astype(BF16)
         AS[b] = (iota((ROWS, ROWS), 1).astype(F32) < block[1:2]).astype(BF16)
-        GF[0, 0, 0, 64 + b : 65 + b] = block[1:2].astype(BF16)
         QA[b, 0:ROWS, ROWS:] = (col == 0).astype(BF16)
         QA[b, ROWS:, ROWS:] = (col == 1).astype(BF16)
         M[b] = jnp.full((8, 256), NEG, F32)
         L[b] = jnp.zeros((8, 256), F32)
         O[b] = jnp.zeros((ROWS, 256), F32)
-    GF[0, 0, 0, 68:72] = jnp.zeros((4, ROWS), BF16)
     out_row, from_row = iota((160, 512), 0), iota((160, 512), 1)
     for h in range(2):
         head = first_head + h
         mid = (out_row >> 5) * ROWS + (out_row & 31) * 4 + head % 4
         far_row = out_row - ROWS
         far = (far_row >> 3) * ROWS + (far_row & 7) * 16 + head
-        SEL[h] = (jnp.where(out_row < ROWS, mid, far) == from_row).astype(BF16)
+        select = (jnp.where(out_row < ROWS, mid, far) == from_row).astype(BF16)
+        SEL[h] = dot(select, PM[...], PLAIN).astype(BF16)
+    for copy in in_cy:
+        copy.wait_recv()
+    CZ[0] = jnp.sum(CY[...], axis=0)
+    in_cz = [
+        send(CZ.at[0], CZ.at[k], cz_s.at[k], cz_r.at[k], at(x, y, (z + k) % NZ))
+        for k in range(1, NZ)
+    ]
     for copy in weights:
         copy.wait()
 
@@ -177,9 +193,8 @@
     in_p[NY - 1].wait_recv()
     project(NY - 1)
 
-    qkv = dot(PM[...], R[...], PLAIN)
-    kv = qkv[:, ROWS:].astype(BF16)
     low = (iota((1, 2 * ROWS), 1) & 127) < 64
+    kv = R[:, ROWS:]
     picked = jnp.where(low, dot(SEL[0], kv, PLAIN), dot(SEL[1], kv, PLAIN)).astype(BF16)
     HM[0, 0, 0:ROWS] = picked[0:ROWS, 0:ROWS]
     HM[0, 0, ROWS:] = picked[0:ROWS, ROWS:]
@@ -200,11 +215,12 @@
     mirror, partner = at(x, y, NZ - 1 - z), at(x, y + 1 - 2 * (y % 2), z)
     order = (10, 11, 9, 14, 6, 2, 8, 3, 1, 12, 4, 7, 13, 15, 5)
     in_far = send(GF.at[0, 0, 0], GF.at[0, 0, 1], gf_s.at[1], gf_r.at[1], mirror)
+    in_near = {o: to_xy(0, o) for o in order}
     in_m01 = middle(0, 1, HM.at[0, 0], mirror)
-    in_near = {o: to_xy(0, o) for o in order}
     in_m10 = middle(1, 0, HM.at[0, 0], partner)
-    KS[...] = kv[:, 0:ROWS]
-    VS[...] = kv[:, ROWS:]
+    qkv = dot(PM[...], R[...], PLAIN)
+    KS[...] = qkv[:, ROWS : 2 * ROWS].astype(BF16)
+    VS[...] = qkv[:, 2 * ROWS :].astype(BF16)
     q32 = qkv[:, 0:ROWS].astype(BF16).astype(F32) * 0.125
     for b in range(SEG):
         q_b = q32[b * ROWS : (b + 1) * ROWS]
@@ -229,47 +245,45 @@
             if finish is not None:
                 finish(b)
 
-    def mask(n, counts, segment_rows, stride):
-        r, c = iota((n, counts.shape[0]), 0), iota((n, counts.shape[0]), 1)
-        per_block = segment_rows // SEG
-        owner = ((r // segment_rows) * 8 + (r % segment_rows) // per_block == c).astype(BF16)
-        position = (iota((n, ROWS), 0) % per_block) * stride
-        position = position + (first_head + jnp.minimum(iota((n, ROWS), 1), 1)) % stride
-        alive = position.astype(F32) < dot(owner, counts, PLAIN)
+    for copy in in_cz:
+        copy.wait_recv()
+    counts = jnp.broadcast_to(jnp.sum(CZ[...], axis=0)[0:1], (ROWS, ROWS)).astype(BF16)
+
+    def mask(n, device, position, stride):
+        owner = (device == iota((n, ROWS), 1)).astype(BF16)
+        head = first_head + jnp.minimum(iota((n, ROWS), 1), 1)
+        position = position * stride + head % stride
+        alive = position.astype(F32) < dot(owner, counts, MINOR)
         return jnp.where(alive, 0.0, NEG).astype(BF16)
 
+    def in_half(f, b):
+        return SEG * (zh + f - 2 * zh * f) + b
+
+    r = iota((512, ROWS), 0)
+    device = (x * NY + (y ^ (r >> 8))) * NZ + in_half((r >> 7) & 1, (r >> 5) & 3)
+    MKM[...] = mask(512, device, r & 31, 4)
+    r = iota((1024, ROWS), 0)
+    device = ((x + NX - ((r >> 7) & 3)) & 3) * NY + ((y + NY - ((r >> 5) & 3)) & 3)
+    MKL[...] = mask(1024, device * NZ + in_half(r >> 9, (r >> 3) & 3), r & 7, 16)
     absorb(KS[...], VS[...], MKS[...])
     in_far.wait_recv()
     in_other = {o: to_xy(1, o) for o in order}
     in_m01.wait_recv()
     in_m11 = middle(1, 1, HM.at[0, 1], partner)
 
-    def whole(dx, f, finish=None):
-        tags = GF[dx : dx + 2, :, f, 64:72].astype(F32).reshape(64, ROWS).astype(BF16)
-        absorb(
-            GF[dx : dx + 2, :, f, 0:LONG].reshape(256, ROWS),
-            GF[dx : dx + 2, :, f, LONG : 2 * LONG].reshape(256, ROWS),
-            mask(256, tags, LONG, 16),
-            finish,
-        )
-
-    for dx in (0, 2):
-        for o in order:
-            if o // NY in (dx, dx + 1):
-                in_near[o].wait_recv()
-        whole(dx, 0)
-    in_other[1].wait_recv()
-    in_other[3].wait_recv()
+    for o in order:
+        in_near[o].wait_recv()
+    absorb(
+        GF[:, :, 0, 0:LONG].reshape(512, ROWS),
+        GF[:, :, 0, LONG:].reshape(512, ROWS),
+        MKL[0:512],
+    )
     in_m10.wait_recv()
     in_m11.wait_recv()
-    tags = [GF[0, 0, 0, 64:72], GF[0, 0, 1, 64:72]]
-    slot = NY - 1 - 2 * (y % 2)
-    tags += [GF[0, slot, 0, 64:72], GF[0, slot, 1, 64:72]]
-    tags = jnp.concatenate([part.astype(F32) for part in tags], axis=0).astype(BF16)
     absorb(
         HM[:, :, 0:ROWS].reshape(512, ROWS),
         HM[:, :, ROWS:].reshape(512, ROWS),
-        mask(512, tags, ROWS, 4),
+        MKM[...],
     )
     backs = []
 
@@ -289,9 +303,14 @@
 
     for dx in (0, 2):
         for o in order:
-            if o // NY in (dx, dx + 1) and o not in (1, 3):
+            if o // NY in (dx, dx + 1):
                 in_other[o].wait_recv()
-        whole(dx, 1, give_back if dx else None)
+        absorb(
+            GF[dx : dx + 2, :, 1, 0:LONG].reshape(256, ROWS),
+            GF[dx : dx + 2, :, 1, LONG:].reshape(256, ROWS),
+            MKL[512 + 128 * dx : 768 + 128 * dx],
+            give_back if dx else None,
+        )
     AT[pair] = AS[zj]
     for g in range(3):
         arrival = remote(AS.at[0], AT.at[g], at_s.at[0], at_r.at[g], sibling)
@@ -332,7 +351,12 @@
         pltpu.VMEM((512, ROWS), BF16),
         pltpu.VMEM((512, ROWS), BF16),
         pltpu.VMEM((512, ROWS), BF16),
-        pltpu.VMEM((NX, NY, 2, 72, ROWS), BF16),
+        pltpu.VMEM((512, ROWS), BF16),
+        pltpu.VMEM((1024, ROWS), BF16),
+        pltpu.VMEM((NX, 8, ROWS), F32),
+        pltpu.VMEM((NY, 8, ROWS), F32),
+        pltpu.VMEM((NZ, 8, ROWS), F32),
+        pltpu.VMEM((NX, NY, 2, 64, ROWS), BF16),
         pltpu.VMEM((2, 2, 256, ROWS), BF16),
         pltpu.VMEM((SEG, 256, 256), BF16),
         pltpu.VMEM((SEG, 8, 256), F32),
@@ -344,7 +368,7 @@
         pltpu.VMEM((ROWS, HALF), F32),
         dma((5,)), dma((3,)), pltpu.SemaphoreType.REGULAR,
     ]
-    for size in (NX, NY * NZ, NY, SEG, NX * NY * 2, 4, SEG, 1):
+    for size in (NX, NY * NZ, NY, SEG, NX * NY * 2, 4, SEG, 1, NX, NY, NZ):
         scratch += [dma((size,)), dma((size,))]
     anywhere = pl.BlockSpec(memory_space=pltpu.HBM)
     own_part, other_part = pl.pallas_call(

time: 50.4 us -> 50.2 us (level)
  no operation moved by 1% of the time
where the time goes in v4:
time: 50.2 us; the launch traced here: 50.1 us
  Pallas kernels  47.8 us (95%)
  other arithmetic  1.65 us (3%)
  between operations  0.66 us (1%)
    pallas_call x1, Pallas kernels, shards(): pl.pallas_call(kernel, out_shape=(jax.ShapeDtypeStruct((ROWS, HALF), F32)...  47.8 us
    convert_element_type x1, other arithmetic, shards(): return (own_part + other_part.astype(F32)).astype(BF16)  1.65 us

profile of v4, /device:TPU:1, one launch (start us, length us, event | category | flops | bytes accessed | tf_op | source)
XLA Modules:
  0.0 50.1 jit_solution(15535626444561252518)
XLA Ops:
  0.7 47.8 %shard_map.64 = (f32[128,384]{1,0:T(8,128)}, bf16[128,384]{1,0:T(8,128)(2,1)}) custom-call(bf16[4,32,384]{2,1,0:T(8,128)(2,1)} %bitcast.5, f32[6,128]{1,0:T(8,128)} %bitcast.6, bf16[3,768,384]{2,1,0:T(8,128)(2,1)} %bitcast.4, bf16[384,768]{1,0:T(8,128)(2,1)} %w_out_in.1, s32[1,128]{1,0:T(1,128)} %bitcast.7, s32[1]{0:T(128)S(6)} %copy.7.cnt_in), custom_call_target="tpu_custom_call" | custom-call | tf_op jit(solution)/shard_map/pallas_call | solution.py:374
  48.4 1.7 %add_convert_fusion = bf16[128,384]{1,0:T(8,128)(2,1)} fusion(f32[128,384]{1,0:T(8,128)} %get-tuple-element.7, bf16[128,384]{1,0:T(8,128)(2,1)} %get-tuple-element.8), kind=kLoop, calls=%fused_computation | loop fusion | flops 147456 | bytes 393216 | tf_op jit(solution)/shard_map/convert_element_type | solution.py:394

commit v5 on v4

--- a/solution.py
+++ b/solution.py
@@ -142,7 +142,6 @@
         PM[b * ROWS : (b + 1) * ROWS] = (wanted == code).astype(BF16)
         alive = place_iota < block[1:2]
         MKS[b * ROWS : (b + 1) * ROWS] = jnp.where(alive, 0.0, NEG).astype(BF16)
-        AS[b] = (iota((ROWS, ROWS), 1).astype(F32) < block[1:2]).astype(BF16)
         QA[b, 0:ROWS, ROWS:] = (col == 0).astype(BF16)
         QA[b, ROWS:, ROWS:] = (col == 1).astype(BF16)
         M[b] = jnp.full((8, 256), NEG, F32)
@@ -215,8 +214,8 @@
     mirror, partner = at(x, y, NZ - 1 - z), at(x, y + 1 - 2 * (y % 2), z)
     order = (10, 11, 9, 14, 6, 2, 8, 3, 1, 12, 4, 7, 13, 15, 5)
     in_far = send(GF.at[0, 0, 0], GF.at[0, 0, 1], gf_s.at[1], gf_r.at[1], mirror)
+    in_m01 = middle(0, 1, HM.at[0, 0], mirror)
     in_near = {o: to_xy(0, o) for o in order}
-    in_m01 = middle(0, 1, HM.at[0, 0], mirror)
     in_m10 = middle(1, 0, HM.at[0, 0], partner)
     qkv = dot(PM[...], R[...], PLAIN)
     KS[...] = qkv[:, ROWS : 2 * ROWS].astype(BF16)
@@ -279,20 +278,24 @@
         MKL[0:512],
     )
     in_m10.wait_recv()
-    in_m11.wait_recv()
+    middles = [HM[0, 0], HM[0, 1], HM[1, 0]]
     absorb(
-        HM[:, :, 0:ROWS].reshape(512, ROWS),
-        HM[:, :, ROWS:].reshape(512, ROWS),
-        MKM[...],
+        jnp.concatenate([part[0:ROWS] for part in middles], axis=0),
+        jnp.concatenate([part[ROWS:] for part in middles], axis=0),
+        MKM[0:384],
     )
     backs = []
+    alive_lanes = [
+        (iota((1, ROWS), 1).astype(F32) < SRC[b][1:2]).astype(F32) for b in range(SEG)
+    ]
 
     def give_back(b):
         halves = []
         for h in range(2):
             cols = slice(h * ROWS, (h + 1) * ROWS)
-            halves.append(O[b][h * 64 : (h + 1) * 64, cols] / L[b][0:1, cols])
-        AS[b] = (jnp.concatenate(halves, axis=0) * AS[b].astype(F32)).astype(BF16)
+            scale = alive_lanes[b] / L[b][0:1, cols]
+            halves.append(O[b][h * 64 : (h + 1) * 64, cols] * scale)
+        AS[b] = jnp.concatenate(halves, axis=0).astype(BF16)
         target = b + zh * (SEG - 1 - 2 * b)
         here = (place == 1) | (place == 2)
         here = here | ((place == 0) & (target == 1)) | ((place == 3) & (target == 2))
@@ -305,30 +308,36 @@
         for o in order:
             if o // NY in (dx, dx + 1):
                 in_other[o].wait_recv()
-        absorb(
-            GF[dx : dx + 2, :, 1, 0:LONG].reshape(256, ROWS),
-            GF[dx : dx + 2, :, 1, LONG:].reshape(256, ROWS),
-            MKL[512 + 128 * dx : 768 + 128 * dx],
-            give_back if dx else None,
-        )
+        keys = GF[dx : dx + 2, :, 1, 0:LONG].reshape(256, ROWS)
+        values = GF[dx : dx + 2, :, 1, LONG:].reshape(256, ROWS)
+        masks = MKL[512 + 128 * dx : 768 + 128 * dx]
+        if dx:
+            in_m11.wait_recv()
+            keys = jnp.concatenate([keys, HM[1, 1, 0:ROWS]], axis=0)
+            values = jnp.concatenate([values, HM[1, 1, ROWS:]], axis=0)
+            masks = jnp.concatenate([masks, MKM[384:]], axis=0)
+        absorb(keys, values, masks, give_back if dx else None)
     AT[pair] = AS[zj]
+    for copy in pending:
+        copy.wait_send()
+    mine = pl.ds(pl.multiple_of(core * HALF, HALF), HALF)
+    other = pl.ds(pl.multiple_of((1 - core) * HALF, HALF), HALF)
+    groups = [slice(g * ROWS, (g + 1) * ROWS) for g in range(3)]
+    for_other = jnp.zeros((ROWS, HALF), F32)
     for g in range(3):
         arrival = remote(AS.at[0], AT.at[g], at_s.at[0], at_r.at[g], sibling)
         pl.when(pair != g)(arrival.wait_recv)
-    attended = AT[...].reshape(HALF, ROWS)
-    mine = pl.ds(pl.multiple_of(core * HALF, HALF), HALF)
-    other = pl.ds(pl.multiple_of((1 - core) * HALF, HALF), HALF)
-    PO[...] = dot(attended, w_out[:, other], MAJOR).astype(BF16)
-    in_o = send(PO, other_part, o_s.at[0], o_r.at[0], sibling)
-    OWN[...] = dot(attended, w_out[:, mine], MAJOR)
+        for_other = for_other + dot(AT[g], w_out[groups[g], other], MAJOR)
+    PO[...] = for_other.astype(BF16)
+    in_o = remote(PO, other_part, o_s.at[0], o_r.at[0], sibling)
+    in_o.start()
+    OWN[...] = dot(AT[...].reshape(HALF, ROWS), w_out[:, mine], MAJOR)
     hand_out = pltpu.make_async_copy(OWN, own_part, loc_sem.at[0])
     hand_out.start()
     hand_out.wait()
-    in_o.wait_recv()
     for copy, here in backs:
         pl.when(here)(copy.wait_send)
-    for copy in pending:
-        copy.wait_send()
+    in_o.wait()
 
 
 def shards(tiles, ln_gain, w_qkv, w_out, tile_source, tissue_count):

time: 50.2 us -> 48.6 us (0.968)
  Pallas kernels: 47.8 us -> 46.1 us
    pallas_call x1, Pallas kernels: 47.8 us -> 46.1 us  [shards(): pl.pallas_call(kernel, out_shape=(jax.ShapeDtypeStruct((ROWS, HALF), F32)...]
where the time goes in v5:
time: 48.6 us; the launch traced here: 48.4 us
  Pallas kernels  46.1 us (95%)
  other arithmetic  1.65 us (3%)
  between operations  0.66 us (1%)
    pallas_call x1, Pallas kernels, shards(): pl.pallas_call(kernel, out_shape=(jax.ShapeDtypeStruct((ROWS, HALF), F32)...  46.1 us
    convert_element_type x1, other arithmetic, shards(): return (own_part + other_part.astype(F32)).astype(BF16)  1.65 us

profile of v5, /device:TPU:1, one launch (start us, length us, event | category | flops | bytes accessed | tf_op | source)
XLA Modules:
  0.0 48.4 jit_solution(16746659702194247432)
XLA Ops:
  0.7 46.1 %shard_map.64 = (f32[128,384]{1,0:T(8,128)}, bf16[128,384]{1,0:T(8,128)(2,1)}) custom-call(bf16[4,32,384]{2,1,0:T(8,128)(2,1)} %bitcast.5, f32[6,128]{1,0:T(8,128)} %bitcast.6, bf16[3,768,384]{2,1,0:T(8,128)(2,1)} %bitcast.4, bf16[384,768]{1,0:T(8,128)(2,1)} %w_out_in.1, s32[1,128]{1,0:T(1,128)} %bitcast.7, s32[1]{0:T(128)S(6)} %copy.7.cnt_in), custom_call_target="tpu_custom_call" | custom-call | tf_op jit(solution)/shard_map/pallas_call | solution.py:383
  46.8 1.7 %add_convert_fusion = bf16[128,384]{1,0:T(8,128)(2,1)} fusion(f32[128,384]{1,0:T(8,128)} %get-tuple-element.7, bf16[128,384]{1,0:T(8,128)(2,1)} %get-tuple-element.8), kind=kLoop, calls=%fused_computation | loop fusion | flops 147456 | bytes 393216 | tf_op jit(solution)/shard_map/convert_element_type | solution.py:403

commit v6 on v5

--- a/solution.py
+++ b/solution.py
@@ -84,21 +84,22 @@
         pl.semaphore_signal(barrier, inc=1, device_id=peer, device_id_type=MESH)
     for copy in small + [own_t] + weights:
         copy.start()
-    for copy in small + [own_t]:
+    own_t.wait()
+    pl.semaphore_wait(barrier, len(peers))
+
+    in_x = [
+        send(T.at[(x + k) % NX], A.at[k], xs_s.at[k], xs_r.at[k], at((x + k) % NX, y, z))
+        for k in range(1, NX)
+    ]
+    for copy in small:
         copy.wait()
     own_count = cnt[0]
     rows8 = iota((8, ROWS), 0)
     tag = jnp.where(rows8 == 0, src[...] // ROWS, own_count)
     SRC[zj] = tag.astype(F32)
     CX[0] = jnp.where(iota((8, ROWS), 1) == seq, own_count, 0).astype(F32)
-    pl.semaphore_wait(barrier, len(peers))
     for peer in y_peers:
         pl.semaphore_signal(ready, inc=1, device_id=peer, device_id_type=MESH)
-
-    in_x = [
-        send(T.at[(x + k) % NX], A.at[k], xs_s.at[k], xs_r.at[k], at((x + k) % NX, y, z))
-        for k in range(1, NX)
-    ]
     in_cx = [
         send(CX.at[0], CX.at[k], cx_s.at[k], cx_r.at[k], at((x + k) % NX, y, z))
         for k in range(1, NX)
@@ -155,13 +156,6 @@
         far = (far_row >> 3) * ROWS + (far_row & 7) * 16 + head
         select = (jnp.where(out_row < ROWS, mid, far) == from_row).astype(BF16)
         SEL[h] = dot(select, PM[...], PLAIN).astype(BF16)
-    for copy in in_cy:
-        copy.wait_recv()
-    CZ[0] = jnp.sum(CY[...], axis=0)
-    in_cz = [
-        send(CZ.at[0], CZ.at[k], cz_s.at[k], cz_r.at[k], at(x, y, (z + k) % NZ))
-        for k in range(1, NZ)
-    ]
     for copy in weights:
         copy.wait()
 
@@ -189,6 +183,14 @@
         if c:
             in_p[c - 1].wait_recv()
             project(c - 1)
+        if c == 1:
+            for copy in in_cy:
+                copy.wait_recv()
+            CZ[0] = jnp.sum(CY[...], axis=0)
+            in_cz = [
+                send(CZ.at[0], CZ.at[k], cz_s.at[k], cz_r.at[k], at(x, y, (z + k) % NZ))
+                for k in range(1, NZ)
+            ]
     in_p[NY - 1].wait_recv()
     project(NY - 1)
 
@@ -244,6 +246,9 @@
             if finish is not None:
                 finish(b)
 
+    absorb(KS[...], VS[...], MKS[...])
+    in_far.wait_recv()
+    in_other = {o: to_xy(1, o) for o in order}
     for copy in in_cz:
         copy.wait_recv()
     counts = jnp.broadcast_to(jnp.sum(CZ[...], axis=0)[0:1], (ROWS, ROWS)).astype(BF16)
@@ -264,9 +269,6 @@
     r = iota((1024, ROWS), 0)
     device = ((x + NX - ((r >> 7) & 3)) & 3) * NY + ((y + NY - ((r >> 5) & 3)) & 3)
     MKL[...] = mask(1024, device * NZ + in_half(r >> 9, (r >> 3) & 3), r & 7, 16)
-    absorb(KS[...], VS[...], MKS[...])
-    in_far.wait_recv()
-    in_other = {o: to_xy(1, o) for o in order}
     in_m01.wait_recv()
     in_m11 = middle(1, 1, HM.at[0, 1], partner)
 

time: 48.6 us -> 48.2 us (level)
  no operation moved by 1% of the time
where the time goes in v6:
time: 48.2 us; the launch traced here: 48.1 us
  Pallas kernels  45.8 us (95%)
  other arithmetic  1.65 us (3%)
  between operations  0.66 us (1%)
    pallas_call x1, Pallas kernels, shards(): pl.pallas_call(kernel, out_shape=(jax.ShapeDtypeStruct((ROWS, HALF), F32)...  45.8 us
    convert_element_type x1, other arithmetic, shards(): return (own_part + other_part.astype(F32)).astype(BF16)  1.65 us

profile of v6, /device:TPU:1, one launch (start us, length us, event | category | flops | bytes accessed | tf_op | source)
XLA Modules:
  0.0 48.1 jit_solution(8742696401454675451)
XLA Ops:
  0.7 45.8 %shard_map.64 = (f32[128,384]{1,0:T(8,128)}, bf16[128,384]{1,0:T(8,128)(2,1)}) custom-call(bf16[4,32,384]{2,1,0:T(8,128)(2,1)} %bitcast.5, f32[6,128]{1,0:T(8,128)} %bitcast.6, bf16[3,768,384]{2,1,0:T(8,128)(2,1)} %bitcast.4, bf16[384,768]{1,0:T(8,128)(2,1)} %w_out_in.1, s32[1,128]{1,0:T(1,128)} %bitcast.7, s32[1]{0:T(128)S(6)} %copy.7.cnt_in), custom_call_target="tpu_custom_call" | custom-call | tf_op jit(solution)/shard_map/pallas_call | solution.py:385
  46.4 1.7 %add_convert_fusion = bf16[128,384]{1,0:T(8,128)(2,1)} fusion(f32[128,384]{1,0:T(8,128)} %get-tuple-element.7, bf16[128,384]{1,0:T(8,128)(2,1)} %get-tuple-element.8), kind=kLoop, calls=%fused_computation | loop fusion | flops 147456 | bytes 393216 | tf_op jit(solution)/shard_map/convert_element_type | solution.py:405

commit v7 on v6

--- a/solution.py
+++ b/solution.py
@@ -77,7 +77,7 @@
     own_t = pltpu.make_async_copy(tiles, T, loc_sem.at[0])
     barrier = pltpu.get_barrier_semaphore()
     peers = [at((x + k) % NX, y, z) for k in range(1, NX)] + [sibling]
-    plane = [(o // NZ, o % NZ) for o in range(1, NY * NZ)]
+    plane = [(dy, dz) for dy in (2, 1, 3, 0) for dz in (4, 3, 5, 2, 6, 1, 7, 0) if dy or dz]
     y_peers = [at(x, (y + k) % NY, z) for k in range(1, NY)]
     peers += y_peers + [at(x, y, (z + k) % NZ) for k in range(1, NZ)]
     for peer in peers:
@@ -163,7 +163,6 @@
     gain_other = jnp.concatenate([gain[pl.ds(3 - 3 * core + i, 1)] for i in range(3)], axis=1)
     w_mine = w_v[pl.ds(pl.multiple_of(core * HALF, HALF), HALF)]
     w_other = w_v[pl.ds(pl.multiple_of((1 - core) * HALF, HALF), HALF)]
-    in_p = []
 
     def project(c):
         a = DD[c].reshape(ROWS, HALF).astype(F32)
@@ -176,14 +175,16 @@
         b = (b * scale * gain_other).astype(BF16)
         R[c * ROWS : (c + 1) * ROWS] = (dot(a, w_mine, PLAIN) + dot(b, w_other, PLAIN)).astype(BF16)
 
-    for c in range(NY):
+    turns = (2, 1, 3, 0)
+    in_p = {}
+    for i, c in enumerate(turns):
         for copy in in_z[c]:
             copy.wait_recv()
-        in_p.append(send(DD.at[c], E.at[c], ps_s.at[c], ps_r.at[c], sibling))
-        if c:
-            in_p[c - 1].wait_recv()
-            project(c - 1)
-        if c == 1:
+        in_p[c] = send(DD.at[c], E.at[c], ps_s.at[c], ps_r.at[c], sibling)
+        if i:
+            in_p[turns[i - 1]].wait_recv()
+            project(turns[i - 1])
+        if i == 1:
             for copy in in_cy:
                 copy.wait_recv()
             CZ[0] = jnp.sum(CY[...], axis=0)
@@ -191,8 +192,8 @@
                 send(CZ.at[0], CZ.at[k], cz_s.at[k], cz_r.at[k], at(x, y, (z + k) % NZ))
                 for k in range(1, NZ)
             ]
-    in_p[NY - 1].wait_recv()
-    project(NY - 1)
+    in_p[turns[-1]].wait_recv()
+    project(turns[-1])
 
     low = (iota((1, 2 * ROWS), 1) & 127) < 64
     kv = R[:, ROWS:]

time: 48.2 us -> 47.4 us (0.983)
  Pallas kernels: 45.8 us -> 44.9 us
    pallas_call x1, Pallas kernels: 45.8 us -> 44.9 us  [shards(): pl.pallas_call(kernel, out_shape=(jax.ShapeDtypeStruct((ROWS, HALF), F32)...]
where the time goes in v7:
time: 47.4 us; the launch traced here: 47.3 us
  Pallas kernels  44.9 us (95%)
  other arithmetic  1.65 us (3%)
  between operations  0.66 us (1%)
    pallas_call x1, Pallas kernels, shards(): pl.pallas_call(kernel, out_shape=(jax.ShapeDtypeStruct((ROWS, HALF), F32)...  44.9 us
    convert_element_type x1, other arithmetic, shards(): return (own_part + other_part.astype(F32)).astype(BF16)  1.65 us

profile of v7, /device:TPU:1, one launch (start us, length us, event | category | flops | bytes accessed | tf_op | source)
XLA Modules:
  0.0 47.3 jit_solution(2464801096650805815)
XLA Ops:
  0.7 44.9 %shard_map.64 = (f32[128,384]{1,0:T(8,128)}, bf16[128,384]{1,0:T(8,128)(2,1)}) custom-call(bf16[4,32,384]{2,1,0:T(8,128)(2,1)} %bitcast.5, f32[6,128]{1,0:T(8,128)} %bitcast.6, bf16[3,768,384]{2,1,0:T(8,128)(2,1)} %bitcast.4, bf16[384,768]{1,0:T(8,128)(2,1)} %w_out_in.1, s32[1,128]{1,0:T(1,128)} %bitcast.7, s32[1]{0:T(128)S(6)} %copy.7.cnt_in), custom_call_target="tpu_custom_call" | custom-call | tf_op jit(solution)/shard_map/pallas_call | solution.py:386
  45.6 1.7 %add_convert_fusion = bf16[128,384]{1,0:T(8,128)(2,1)} fusion(f32[128,384]{1,0:T(8,128)} %get-tuple-element.7, bf16[128,384]{1,0:T(8,128)(2,1)} %get-tuple-element.8), kind=kLoop, calls=%fused_computation | loop fusion | flops 147456 | bytes 393216 | tf_op jit(solution)/shard_map/convert_element_type | solution.py:406

commit v8 on v7

--- a/solution.py
+++ b/solution.py
@@ -215,7 +215,7 @@
         return send(source, HM.at[yy, f], hm_s.at[o], hm_r.at[o], device)
 
     mirror, partner = at(x, y, NZ - 1 - z), at(x, y + 1 - 2 * (y % 2), z)
-    order = (10, 11, 9, 14, 6, 2, 8, 3, 1, 12, 4, 7, 13, 15, 5)
+    order = (10, 6, 14, 2, 9, 11, 8, 5, 7, 13, 15, 1, 3, 4, 12)
     in_far = send(GF.at[0, 0, 0], GF.at[0, 0, 1], gf_s.at[1], gf_r.at[1], mirror)
     in_m01 = middle(0, 1, HM.at[0, 0], mirror)
     in_near = {o: to_xy(0, o) for o in order}

time: 47.4 us -> 47.1 us (level)
  no operation moved by 1% of the time
where the time goes in v8:
time: 47.1 us; the launch traced here: 47 us
  Pallas kernels  44.7 us (95%)
  other arithmetic  1.65 us (4%)
  between operations  0.66 us (1%)
    pallas_call x1, Pallas kernels, shards(): pl.pallas_call(kernel, out_shape=(jax.ShapeDtypeStruct((ROWS, HALF), F32)...  44.7 us
    convert_element_type x1, other arithmetic, shards(): return (own_part + other_part.astype(F32)).astype(BF16)  1.65 us

profile of v8, /device:TPU:1, one launch (start us, length us, event | category | flops | bytes accessed | tf_op | source)
XLA Modules:
  0.0 47.0 jit_solution(10922520357725557342)
XLA Ops:
  0.7 44.7 %shard_map.64 = (f32[128,384]{1,0:T(8,128)}, bf16[128,384]{1,0:T(8,128)(2,1)}) custom-call(bf16[4,32,384]{2,1,0:T(8,128)(2,1)} %bitcast.5, f32[6,128]{1,0:T(8,128)} %bitcast.6, bf16[3,768,384]{2,1,0:T(8,128)(2,1)} %bitcast.4, bf16[384,768]{1,0:T(8,128)(2,1)} %w_out_in.1, s32[1,128]{1,0:T(1,128)} %bitcast.7, s32[1]{0:T(128)S(6)} %copy.7.cnt_in), custom_call_target="tpu_custom_call" | custom-call | tf_op jit(solution)/shard_map/pallas_call | solution.py:386
  45.4 1.7 %add_convert_fusion = bf16[128,384]{1,0:T(8,128)(2,1)} fusion(f32[128,384]{1,0:T(8,128)} %get-tuple-element.7, bf16[128,384]{1,0:T(8,128)(2,1)} %get-tuple-element.8), kind=kLoop, calls=%fused_computation | loop fusion | flops 147456 | bytes 393216 | tf_op jit(solution)/shard_map/convert_element_type | solution.py:406
